TPU v7x, 256 devices: a whole 4x4x8 slice. The times are simulated.
256 devices in a mesh: row: 16 (over y, x), col: 16 (over z, core).
Axes of the slice: x: 4, y: 4, z: 8, core: 2. Of those that a mesh axis runs over, the one named last changes fastest.
Arguments:
- inputs: bfloat16 [512, 8192], P('col', 'row'), may hold values from -6 to 6
- gate_weight: bfloat16 [8192, 28672], P('row', 'col'), may hold values from -0.0625 to 0.0625
- up_weight: bfloat16 [8192, 28672], P('row', 'col'), may hold values from -0.0625 to 0.0625
- down_weight: bfloat16 [28672, 8192], P('col', 'row'), may hold values from -0.03125 to 0.03125
- out_grad: bfloat16 [512, 8192], P('col', 'row'), may hold values from -1.5 to 1.5
Outputs:
- output: bfloat16 [512, 8192], P('col', 'row')
- in_grad: bfloat16 [512, 8192], P('col', 'row')
- gate_grad: bfloat16 [8192, 28672], P('row', 'col')
- up_grad: bfloat16 [8192, 28672], P('row', 'col')
- down_grad: bfloat16 [28672, 8192], P('col', 'row')
All inputs are finite; a program needn't handle non-finite values.
Results may differ from a plain program's by a relative error of at most 0.005.
Values may be sent and summed in bfloat16 or wider, within the bound.
No kernel may reach another device: no remote copies, remote signals or barrier semaphores. Data moves between devices by JAX's collectives and lax.ppermute only.
A program may use at most 128 MiB of HBM per device.

v0:
```python
import jax
import jax.numpy as jnp
from jax import lax
from jax.sharding import PartitionSpec as P


def contract_first(left, right):
    return lax.dot_general(
        left, right, (((0,), (0,)), ((), ())), preferred_element_type=jnp.float32
    )


def contract_last(left, right):
    return lax.dot_general(
        left, right, (((1,), (1,)), ((), ())), preferred_element_type=jnp.float32
    )


def gating(gate_value, up_value):
    sigmoid_gate = jax.nn.sigmoid(gate_value)
    return (gate_value * sigmoid_gate * up_value).astype(jnp.bfloat16)


def gating_grads(hidden_grad, gate_value, up_value):
    sigmoid_gate = jax.nn.sigmoid(gate_value)
    slope = sigmoid_gate * (1.0 + gate_value * (1.0 - sigmoid_gate))
    gate_part = (hidden_grad * up_value * slope).astype(jnp.bfloat16)
    up_part = (hidden_grad * gate_value * sigmoid_gate).astype(jnp.bfloat16)
    return (gate_part, up_part)


def on_device(inputs, gate_weight, up_weight, down_weight, out_grad):
    all_inputs, all_grads = (
        lax.all_gather(inputs, "col", axis=0, tiled=True),
        lax.all_gather(out_grad, "col", axis=0, tiled=True),
    )
    gate_value, up_value = lax.psum(
        (
            jnp.dot(all_inputs, gate_weight, preferred_element_type=jnp.float32),
            jnp.dot(all_inputs, up_weight, preferred_element_type=jnp.float32),
        ),
        "row",
    )
    hidden = gating(gate_value, up_value)
    hidden_grad = lax.psum(contract_last(all_grads, down_weight), "row")
    gate_part, up_part = gating_grads(hidden_grad, gate_value, up_value)
    output = lax.psum_scatter(
        jnp.dot(hidden, down_weight, preferred_element_type=jnp.float32),
        "col",
        scatter_dimension=0,
        tiled=True,
    ).astype(jnp.bfloat16)
    in_grad = lax.psum_scatter(
        contract_last(gate_part, gate_weight) + contract_last(up_part, up_weight),
        "col",
        scatter_dimension=0,
        tiled=True,
    ).astype(jnp.bfloat16)
    gate_grad = contract_first(all_inputs, gate_part).astype(jnp.bfloat16)
    up_grad = contract_first(all_inputs, up_part).astype(jnp.bfloat16)
    down_grad = contract_first(hidden, all_grads).astype(jnp.bfloat16)
    return (output, in_grad, gate_grad, up_grad, down_grad)


def solution(mesh):
    in_specs = (P("col", "row"), P("row", "col"), P("row", "col"), P("col", "row"), P("col", "row"))
    out_specs = (
        P("col", "row"),
        P("col", "row"),
        P("row", "col"),
        P("row", "col"),
        P("col", "row"),
    )
    return jax.shard_map(
        on_device, mesh=mesh, in_specs=in_specs, out_specs=out_specs, check_vma=False
    )
```

profile of v0, /device:TPU:2, one launch (start us, length us, event | category | flops | bytes accessed | tf_op | source)
XLA Modules:
  0.0 365.2 jit_solution(4392289032627727677)
XLA Ops:
  7.2 0.0 copy-start
  7.2 0.0 all-reduce.3.cloned.1.call-start
  7.2 21.8 %all_gather.6 = bf16[512,512]{1,0:T(8,128)(2,1)S(1)} all-gather(bf16[32,512]{1,0:T(8,128)(2,1)} %param.5), channel_id=1, replica_groups=mesh['row'=16,'col'=16] {'col'}, dimensions={0}, use_global_device_ids=true | all-gather | bytes 557056 | tf_op jit(solution)/shard_map/all_gather | solution.py:34
  29.0 16.1 %all_gather.7 = bf16[512,512]{1,0:T(8,128)(2,1)S(1)} all-gather(bf16[32,512]{1,0:T(8,128)(2,1)} %param.9), channel_id=1, replica_groups=mesh['row'=16,'col'=16] {'col'}, dimensions={0}, use_global_device_ids=true | all-gather | bytes 557056 | tf_op jit(solution)/shard_map/all_gather | solution.py:35
  45.1 4.5 %fusion.3 = f32[512,1792]{1,0:T(8,128)} fusion(bf16[512,512]{1,0:T(8,128)(2,1)S(1)} %all_gather.6, bf16[512,1792]{1,0:T(8,128)(2,1)} %param.7), kind=kOutput, calls=%fused_computation.11 | convolution fusion | flops 939524096 | bytes 6029312 | tf_op jit(solution)/shard_map/dot_general | solution.py:40
  49.7 0.0 copy-done
  49.7 0.0 copy-start.2
  49.7 2.9 fusion.2
  52.6 0.0 copy-done.2
  52.6 3.0 fusion.5
  55.5 0.0 all-reduce.3.cloned.1.call-update
  55.6 0.0 reduce-scatter.5.cloned.1.call-start
  55.6 172.9 %all-reduce.3.cloned.1.call-done = (f32[512,1792]{1,0:T(8,128)}, f32[512,1792]{1,0:T(8,128)}, f32[512,1792]{1,0:T(8,128)}) async-done(((f32[512,1792]{1,0:T(8,128)}, f32[512,1792]{1,0:T(8,128)}, f32[512,1792]{1,0:T(8,128)}), (f32[512,1792]{1,0:T(8,128)}, f32[512,1792]{1,0:T(8,128)}, f32[512,1792]{1,0:T(8,128)})) %all-reduce.3.cloned.1.call-update) | async-done | bytes 11010064 | tf_op jit(solution)/shard_map/psum | solution.py:37
  228.5 6.2 %multiply_convert_fusion = (bf16[512,1792]{1,0:T(8,128)(2,1)S(1)}, bf16[512,1792]{1,0:T(8,128)(2,1)S(1)}, bf16[512,1792]{1,0:T(8,128)(2,1)}) fusion(f32[512,1792]{1,0:T(8,128)} %get-tuple-element.12, f32[512,1792]{1,0:T(8,128)} %get-tuple-element.11, f32[512,1792]{1,0:T(8,128)} %get-tuple-element.10), kind=kLoop, calls=%fused_computation | loop fusion | flops 14680064 | bytes 16515072 | tf_op jit(solution)/shard_map/convert_element_type | solution.py:28
  234.8 0.0 copy-start.4
  234.8 0.0 copy-start.3
  234.8 0.0 copy-start.1
  234.8 1.1 fusion.6
  235.9 0.1 copy-done.4
  236.0 0.6 copy-done.3
  236.7 1.0 copy-done.1
  237.6 2.1 convolution_add_fusion
  239.7 0.0 reduce-scatter.5.cloned.1.call-update
  239.8 0.0 reduce-scatter.3.cloned.1.call-start
  239.8 4.1 %fusion.4 = f32[512,512]{1,0:T(8,128)} fusion(bf16[512,1792]{1,0:T(8,128)(2,1)} %get-tuple-element.15, bf16[1792,512]{1,0:T(8,128)(2,1)} %param.8), kind=kOutput, calls=%fused_computation.12 | convolution fusion | flops 939524096 | bytes 4718592 | tf_op jit(solution)/shard_map/dot_general | solution.py:48
  244.0 0.0 reduce-scatter.3.cloned.1.call-update
  244.0 3.9 %fusion = bf16[512,1792]{0,1:T(8,128)(2,1)} fusion(bf16[512,1792]{1,0:T(8,128)(2,1)} %copy-done.4, bf16[512,512]{1,0:T(8,128)(2,1)S(1)} %all_gather.6), kind=kOutput, calls=%fused_computation.7 | convolution fusion | flops 940441600 | bytes 4194304 | tf_op jit(solution)/shard_map/dot_general | solution.py:8
  247.9 3.8 %copy.10 = bf16[512,1792]{1,0:T(8,128)(2,1)} copy(bf16[512,1792]{0,1:T(8,128)(2,1)} %fusion) | data formatting | bytes 3670016
  251.7 3.9 %fusion.1 = bf16[512,1792]{0,1:T(8,128)(2,1)} fusion(bf16[512,1792]{1,0:T(8,128)(2,1)} %copy-done.3, bf16[512,512]{1,0:T(8,128)(2,1)S(1)} %all_gather.6), kind=kOutput, calls=%fused_computation.8 | convolution fusion | flops 940441600 | bytes 4194304 | tf_op jit(solution)/shard_map/dot_general | solution.py:8
  255.5 3.8 %copy.11 = bf16[512,1792]{1,0:T(8,128)(2,1)} copy(bf16[512,1792]{0,1:T(8,128)(2,1)} %fusion.1) | data formatting | bytes 3670016
  259.4 3.9 %convolution_convert_fusion = bf16[1792,512]{1,0:T(8,128)(2,1)} fusion(bf16[512,1792]{1,0:T(8,128)(2,1)} %get-tuple-element.15, bf16[512,512]{1,0:T(8,128)(2,1)S(1)} %all_gather.7), kind=kOutput, calls=%fused_computation.4 | convolution fusion | flops 940441600 | bytes 4194304 | tf_op jit(solution)/shard_map/dot_general | solution.py:8
  263.2 34.6 %reduce-scatter.5.cloned.1.call-done = f32[32,512]{1,0:T(8,128)} async-done(((f32[512,512]{1,0:T(8,128)}), f32[32,512]{1,0:T(8,128)}) %reduce-scatter.5.cloned.1.call-update) | async-done | bytes 65552 | tf_op jit(solution)/shard_map/reduce_scatter | solution.py:53
  297.9 1.5 convert_element_type.34
  299.3 57.9 %reduce-scatter.3.cloned.1.call-done = f32[32,512]{1,0:T(8,128)} async-done(((f32[512,512]{1,0:T(8,128)}), f32[32,512]{1,0:T(8,128)}) %reduce-scatter.3.cloned.1.call-update) | async-done | bytes 65552 | tf_op jit(solution)/shard_map/reduce_scatter | solution.py:47
  357.3 1.5 convert_element_type.31
Async XLA Ops:
  7.2 42.5 %copy-start = (bf16[512,1792]{1,0:T(8,128)(2,1)S(1)}, bf16[512,1792]{1,0:T(8,128)(2,1)}, u32[]{:S(2)}) copy-start(bf16[512,1792]{1,0:T(8,128)(2,1)} %param.6) | copy-start | bytes 5505028
  7.2 221.4 %all-reduce.3.cloned.1.call-start = ((), (), s32[]{:S(2)}) async-start(), calls=%async_computation.4 | async-start | bytes 22020096 | tf_op jit(solution)/shard_map/psum | solution.py:37
  49.7 2.9 copy-start.2
  55.6 242.3 %reduce-scatter.5.cloned.1.call-start = ((), (), s32[]{:S(2)}) async-start(), calls=%async_computation.3 | async-start | bytes 1114112 | tf_op jit(solution)/shard_map/reduce_scatter | solution.py:53
  234.8 1.2 copy-start.4
  234.8 1.9 copy-start.3
  234.8 2.8 copy-start.1
  239.8 117.5 %reduce-scatter.3.cloned.1.call-start = ((), (), s32[]{:S(2)}) async-start(), calls=%async_computation.2 | async-start | bytes 1114112 | tf_op jit(solution)/shard_map/reduce_scatter | solution.py:47
Sparse Core Ops, SparseCore 0:
  55.7 172.8 all-reduce.2
  239.9 57.9 reduce-scatter.4
  300.4 56.8 reduce-scatter.2
where the time goes:
time: 366 us; the launch traced here: 365 us
  waiting for transfers between devices  266 us (73%)
  blocking collectives  37.9 us (10%)
  matrix products  29.4 us (8%)
  between operations  13.8 us (4%)
  local copies, waits for them, and re-layouts  9.29 us (3%)
  other arithmetic  9.16 us (3%)
    psum x1, waiting for transfers between devices, on_device(): lax.psum((jnp.dot(all_inputs, gate_weight, preferred_element_type=jnp.flo...  173 us
    reduce_scatter x1, waiting for transfers between devices, on_device(): lax.psum_scatter(jnp.dot(hidden, down_weight, preferred_element_type=jnp....  57.9 us
    reduce_scatter x1, waiting for transfers between devices, on_device(): lax.psum_scatter(contract_last(gate_part, gate_weight) + contract_last(up...  34.6 us
    all_gather x1, blocking collectives, on_device(): lax.all_gather(inputs, 'col', axis=0, tiled=True)  21.8 us
    all_gather x1, blocking collectives, on_device(): lax.all_gather(out_grad, 'col', axis=0, tiled=True)  16.1 us
    dot_general x3, matrix products, contract_first(): lax.dot_general(left, right, (((0,), (0,)), ((), ())), preferred_element_...  11.6 us
    unnamed x12, local copies, waits for them, and re-layouts  9.29 us
  transfers between devices with their start and end apart: 3, of which 3 were waited for; matrix products, arithmetic and copies ran while one was open for 7% of the time, Pallas kernels for 0%

commit v1 on v0

v1 whole, which is shorter than its diff:
```python
import functools

import jax
import jax.numpy as jnp
from jax import lax
from jax.experimental import pallas as pl
from jax.experimental.pallas import tpu as pltpu
from jax.sharding import PartitionSpec as P


BF16, F32 = jnp.bfloat16, jnp.float32
SIDE = 4
DEEP = 8
BLOCKS = 16
VMEM_LIMIT = 56 * 1024 * 1024


def contract(left, right, left_dim, right_dim):
    return lax.dot_general(
        left, right, (((left_dim,), (right_dim,)), ((), ())), preferred_element_type=F32
    )


def shift(k, along):
    pairs = []
    for y in range(SIDE):
        for x in range(SIDE):
            for c in range(2 * DEEP):
                dy, dx = along if c % 2 == 0 else along[::-1]
                row = (y + k * dy) % SIDE * SIDE + (x + k * dx) % SIDE
                pairs.append(((y * SIDE + x) * 2 * DEEP + c, row * 2 * DEEP + c))
    return pairs


MAJOR, MINOR = (0, 1), (1, 0)


def partner():
    return [(c, c ^ 1) for c in range(2 * DEEP)]


def call(kernel, outs, n_scalar, args, scratch=()):
    vmem = pl.BlockSpec(memory_space=pltpu.VMEM)
    smem = pl.BlockSpec(memory_space=pltpu.SMEM)
    return pl.pallas_call(
        kernel,
        out_shape=[jax.ShapeDtypeStruct(s, d) for s, d in outs],
        in_specs=[smem] * n_scalar + [vmem] * (len(args) - n_scalar),
        out_specs=[vmem] * len(outs),
        scratch_shapes=scratch,
        compiler_params=pltpu.CompilerParams(vmem_limit_bytes=VMEM_LIMIT),
    )(*args)


def take_blocks(order, source, target):
    rows = source.shape[0] // BLOCKS
    for s in range(BLOCKS):
        at = pl.ds(pl.multiple_of(order[s] * rows, rows), rows)
        target[s * rows : (s + 1) * rows] = source[at, :]


def partial_kernel(dim, order, left, *refs):
    *weights, keep, send1, send2, send3, mine = refs
    take_blocks(order, left, mine)
    group = keep.shape[1]
    for n, weight in enumerate(weights):
        value = contract(mine[...], weight[...], 1, dim)
        keep[n] = value[:group]
        for k, send in enumerate((send1, send2, send3)):
            send[n] = value[(k + 1) * group : (k + 2) * group].astype(BF16)


def first_sum_kernel(keep_gu, keep_h, *refs):
    got_gu, got_h, outs = refs[:3], refs[3:6], refs[6:]
    rows = outs[0].shape[1]
    for k, out in enumerate(outs):
        at = slice(k * rows, (k + 1) * rows)
        for keep, gots, lo in ((keep_gu, got_gu, 0), (keep_h, got_h, 2)):
            total = keep[:, at, :]
            for got in gots:
                total = total + got[:, at, :].astype(F32)
            out[lo : lo + keep.shape[0]] = total.astype(out.dtype)


def gating_kernel(own, got1, got2, got3, out):
    gate, up, grad = (
        own[n] + got1[n].astype(F32) + got2[n].astype(F32) + got3[n].astype(F32)
        for n in range(3)
    )
    sig = jax.nn.sigmoid(gate)
    out[0] = (gate * sig * up).astype(BF16)
    out[1] = (grad * up * (sig * (1.0 + gate * (1.0 - sig)))).astype(BF16)
    out[2] = (grad * gate * sig).astype(BF16)


def join_kernel(*refs):
    blocks, outs = refs[: SIDE - 1], refs[SIDE - 1 :]
    rows = blocks[0].shape[1]
    for k, block in enumerate(blocks):
        at = slice(k * rows, (k + 1) * rows)
        lo = 0
        for out in outs:
            n = out.shape[0]
            out[:, at, :] = block[lo : lo + n]
            lo += n


def stack_rows(shards, n, rests, m, target):
    rows, more = shards[0].shape[1], rests[0].shape[1]
    for k, (shard, rest) in enumerate(zip(shards, rests)):
        at = k * (rows + more)
        target[at : at + rows] = shard[n]
        target[at + rows : at + rows + more] = rest[m]


def product_kernel(dim, first, place, *refs):
    shards, rests, weights = refs[:SIDE], refs[SIDE : 2 * SIDE], refs[2 * SIDE : -4]
    mine, theirs, total, stack = refs[-4:]
    tokens = stack.shape[0]
    rows = tokens // BLOCKS
    value = None
    for n, weight in enumerate(weights):
        stack_rows(shards, first + n, rests, n, stack)
        term = contract(stack[...], weight[...], 1, dim)
        value = term if value is None else value + term
    for s in range(BLOCKS):
        at = pl.ds(pl.multiple_of(place[s] * rows, rows), rows)
        total[at, :] = value[s * rows : (s + 1) * rows]
    mine[...] = total[: tokens // 2]
    theirs[...] = total[tokens // 2 :]


def down_grad_kernel(order, og, *refs):
    shards, rests = refs[:SIDE], refs[SIDE : 2 * SIDE]
    down_grad, mine, stack = refs[2 * SIDE :]
    take_blocks(order, og, mine)
    stack_rows(shards, 0, rests, 0, stack)
    down_grad[...] = contract(stack[...], mine[...], 0, 0).astype(BF16)


def weight_grads_kernel(order, x, *refs):
    shards, rests = refs[:SIDE], refs[SIDE : 2 * SIDE]
    gate_grad, up_grad, mine, stack = refs[2 * SIDE :]
    take_blocks(order, x, mine)
    for n, grad in enumerate((gate_grad, up_grad)):
        stack_rows(shards, 1 + n, rests, n, stack)
        grad[...] = contract(mine[...], stack[...], 0, 0).astype(BF16)


def send(value, k, along):
    return lax.ppermute(value, ("row", "col"), shift(k, along))


def spread(values, along):
    return [send(v, k + 1, along) for k, v in enumerate(values)]


def collect(value, along):
    return [value] + [send(value, -k, along) for k in range(1, SIDE)]


def z_reduce(mine, theirs, wire, same_core):
    total = (mine + lax.ppermute(theirs, "col", partner())).astype(wire)
    got = lax.all_to_all(total, "col", 0, 0, axis_index_groups=same_core, tiled=True)
    return jnp.sum(got.reshape(DEEP, -1, got.shape[1]).astype(F32), axis=0).astype(BF16)


def on_device(inputs, gate_weight, up_weight, down_weight, out_grad):
    deep, width = gate_weight.shape
    row, col = lax.axis_index("row"), lax.axis_index("col")
    y, x, core = row // SIDE, row % SIDE, col % 2
    slot = jnp.arange(BLOCKS, dtype=jnp.int32)
    outer, inner = slot // SIDE, slot % SIDE
    dy, dx = jnp.where(core == 0, inner, outer), jnp.where(core == 0, outer, inner)
    order = (y + dy) % SIDE * SIDE + (x + dx) % SIDE
    place = (order + core) % 2 * DEEP + order // 2
    same_core = [[2 * z + c for z in range(DEEP)] for c in range(2)]

    all_inputs = lax.all_gather(inputs, "col", axis=0, tiled=True)
    tokens = all_inputs.shape[0]
    rows = tokens // BLOCKS
    group = SIDE * rows

    def partials(left, weights, dim):
        n = len(weights)
        return call(
            functools.partial(partial_kernel, dim),
            [((n, group, width), F32)] + [((n, group, width), BF16)] * 3,
            1,
            (order, left, *weights),
            [pltpu.VMEM((tokens, deep), BF16)],
        )

    def product(pieces, weights, dim, first):
        return call(
            functools.partial(product_kernel, dim, first),
            [((tokens // 2, deep), F32)] * 2,
            1,
            (place, *pieces, *weights),
            [pltpu.VMEM((tokens, deep), F32), pltpu.VMEM((tokens, width), BF16)],
        )

    keep_gu, *sends = partials(all_inputs, (gate_weight, up_weight), 0)
    got_gu = spread(sends, MAJOR)
    out_grad, keep_gu = lax.optimization_barrier((out_grad, keep_gu))
    all_grads = lax.all_gather(out_grad, "col", axis=0, tiled=True)
    keep_h, *sends = partials(all_grads, (down_weight,), 1)
    got_h = spread(sends, MAJOR)
    own, *sends = call(
        first_sum_kernel,
        [((3, rows, width), F32)] + [((3, rows, width), BF16)] * 3,
        0,
        (keep_gu, keep_h, *got_gu, *got_h),
    )
    (shard,) = call(
        gating_kernel, [((3, rows, width), BF16)], 0, (own, *spread(sends, MINOR))
    )
    blocks = collect(shard, MINOR)[1:]
    shards = collect(shard, MAJOR)
    more = (SIDE - 1) * rows
    hidden, parts = call(
        join_kernel, [((1, more, width), BF16), ((2, more, width), BF16)], 0, blocks
    )
    hiddens = shards + collect(hidden, MAJOR)
    grads = shards + collect(parts, MAJOR)

    scratch = [pltpu.VMEM((tokens, deep), BF16), pltpu.VMEM((tokens, width), BF16)]
    sums = product(hiddens, (down_weight,), 0, 0)
    output = z_reduce(*sums, BF16, same_core)
    (down_grad,) = call(
        down_grad_kernel, [((width, deep), BF16)], 1,
        (order, all_grads, *hiddens), scratch,
    )
    sums = product(grads, (gate_weight, up_weight), 1, 1)
    in_grad = z_reduce(*sums, BF16, same_core)
    gate_grad, up_grad = call(
        weight_grads_kernel, [((deep, width), BF16)] * 2, 1,
        (order, all_inputs, *grads), scratch,
    )
    return (output, in_grad, gate_grad, up_grad, down_grad)


def solution(mesh):
    in_specs = (P("col", "row"), P("row", "col"), P("row", "col"), P("col", "row"), P("col", "row"))
    out_specs = (
        P("col", "row"),
        P("col", "row"),
        P("row", "col"),
        P("row", "col"),
        P("col", "row"),
    )
    return jax.shard_map(
        on_device, mesh=mesh, in_specs=in_specs, out_specs=out_specs, check_vma=False
    )
```

time: 366 us -> 209 us (0.57)
  waiting for transfers between devices: 266 us -> 80 us
  Pallas kernels: 0 us -> 40.1 us
  starting transfers between devices: 0.12 us -> 36.9 us
  matrix products: 29.4 us -> 0 us
  between operations: 13.8 us -> 0.83 us
  other arithmetic: 9.16 us -> 3.39 us
  local copies, waits for them, and re-layouts: 9.29 us -> 4.8 us
    psum x1 -> x0, waiting for transfers between devices: 173 us -> none  [on_device(): lax.psum((jnp.dot(all_inputs, gate_weight, preferred_element_type=jnp.flo...]
    reduce_scatter x2 -> x0, waiting for transfers between devices: 92.6 us -> none  [the longest x1 57.9 us: on_device(): lax.psum_scatter(jnp.dot(hidden, down_weight, preferred_element_type=jnp....]
    ppermute x0 -> x23, waiting for transfers between devices: none -> 66.7 us  [the longest x21 66.7 us: send(): return lax.ppermute(value, ('row', 'col'), shift(k, along))]
    pallas_call x0 -> x9, Pallas kernels: none -> 40.1 us  [call(): pl.pallas_call(kernel, out_shape=[jax.ShapeDtypeStruct(s, d) for s, d in...]
    dot_general x9 -> x0, matrix products: 29.4 us -> none  [the longest x3 11.6 us: contract_first(): lax.dot_general(left, right, (((0,), (0,)), ((), ())), preferred_element_...]
    ppermute x0 -> x23, starting transfers between devices: none -> 29 us  [the longest x21 29 us: send(): return lax.ppermute(value, ('row', 'col'), shift(k, along))]
    all_to_all x0 -> x2, waiting for transfers between devices: none -> 13.2 us  [z_reduce(): lax.all_to_all(total, 'col', 0, 0, axis_index_groups=same_core, tiled=True)]
    all_to_all x0 -> x2, starting transfers between devices: none -> 7.89 us  [z_reduce(): lax.all_to_all(total, 'col', 0, 0, axis_index_groups=same_core, tiled=True)]
  transfers between devices with their start and end apart: 3 -> 25, of which waited for: 3 -> 15; matrix products, arithmetic and copies ran while one was open for 7% -> 1% of each run, Pallas kernels for 0% -> 11%
where the time goes in v1:
time: 209 us; the launch traced here: 207 us
  waiting for transfers between devices  80 us (38%)
  blocking collectives  40.5 us (19%)
  Pallas kernels  40.1 us (19%)
  starting transfers between devices  36.9 us (18%)
  local copies, waits for them, and re-layouts  4.8 us (2%)
  other arithmetic  3.39 us (2%)
    ppermute x21, waiting for transfers between devices, send(): return lax.ppermute(value, ('row', 'col'), shift(k, along))  66.7 us
    pallas_call x9, Pallas kernels, call(): pl.pallas_call(kernel, out_shape=[jax.ShapeDtypeStruct(s, d) for s, d in...  40.1 us
    ppermute x21, starting transfers between devices, send(): return lax.ppermute(value, ('row', 'col'), shift(k, along))  29 us
    all_gather x1, blocking collectives, on_device(): all_inputs = lax.all_gather(inputs, 'col', axis=0, tiled=True)  23.1 us
    all_gather x1, blocking collectives, on_device(): all_grads = lax.all_gather(out_grad, 'col', axis=0, tiled=True)  17.4 us
    all_to_all x2, waiting for transfers between devices, z_reduce(): lax.all_to_all(total, 'col', 0, 0, axis_index_groups=same_core, tiled=True)  13.2 us
    all_to_all x2, starting transfers between devices, z_reduce(): lax.all_to_all(total, 'col', 0, 0, axis_index_groups=same_core, tiled=True)  7.89 us
    unnamed x54, local copies, waits for them, and re-layouts  4.8 us
  transfers between devices with their start and end apart: 25, of which 15 were waited for; matrix products, arithmetic and copies ran while one was open for 1% of the time, Pallas kernels for 11%

profile of v1, /device:TPU:2, one launch (start us, length us, event | category | flops | bytes accessed | tf_op | source)
XLA Modules:
  0.0 206.5 jit_solution(4687196214525705164)
XLA Ops:
  0.7 23.1 %all_gather.6.left.x = bf16[512,512]{1,0:T(8,128)(2,1)} all-gather(bf16[32,512]{1,0:T(8,128)(2,1)} %param.5), channel_id=1, replica_groups=mesh['row'=16,'col'=16] {'col'}, dimensions={0}, use_global_device_ids=true | all-gather | bytes 557056 | tf_op jit(solution)/shard_map/all_gather | solution.py:179
  24.2 6.3 %shard_map.92 = (f32[2,128,1792]{2,1,0:T(8,128)}, bf16[2,128,1792]{2,1,0:T(8,128)(2,1)}, bf16[2,128,1792]{2,1,0:T(8,128)(2,1)}, bf16[2,128,1792]{2,1,0:T(8,128)(2,1)}) custom-call(s32[16]{0:T(128)} %get-tuple-element.50.order, bf16[512,512]{1,0:T(8,128)(2,1)} %all_gather.6.left.x, bf16[512,1792]{1,0:T(8,128)(2,1)} %refs_8_.3, bf16[512,1792]{1,0:T(8,128)(2,1)} %refs_9_.1), custom_call_target="tpu_custom_call" | custom-call | tf_op jit(solution)/shard_map/pallas_call | solution.py:45
  30.6 17.4 %all_gather.7.left.og = bf16[512,512]{1,0:T(8,128)(2,1)} all-gather(bf16[32,512]{1,0:T(8,128)(2,1)S(1)} %copy-done.23), channel_id=1, replica_groups=mesh['row'=16,'col'=16] {'col'}, dimensions={0}, use_global_device_ids=true | all-gather | bytes 557056 | tf_op jit(solution)/shard_map/all_gather | solution.py:206
  48.0 4.1 %shard_map.93 = (f32[1,128,1792]{2,1,0:T(8,128)}, bf16[1,128,1792]{2,1,0:T(8,128)(2,1)}, bf16[1,128,1792]{2,1,0:T(8,128)(2,1)}, bf16[1,128,1792]{2,1,0:T(8,128)(2,1)}) custom-call(s32[16]{0:T(128)} %get-tuple-element.50.order, bf16[512,512]{1,0:T(8,128)(2,1)} %all_gather.7.left.og, bf16[1792,512]{1,0:T(8,128)(2,1)} %refs_8_.2), custom_call_target="tpu_custom_call" | custom-call | tf_op jit(solution)/shard_map/pallas_call | solution.py:45
  52.2 1.5 collective-permute-start.3
  53.7 1.2 collective-permute-start
  54.9 1.4 collective-permute-start.1
  56.3 1.1 collective-permute-start.2
  57.4 1.2 collective-permute-start.4
  58.6 2.2 %collective-permute-done.3.refs_3_ = bf16[1,128,1792]{2,1,0:T(8,128)(2,1)S(1)} collective-permute-done((bf16[1,128,1792]{2,1,0:T(8,128)(2,1)}, bf16[1,128,1792]{2,1,0:T(8,128)(2,1)S(1)}, u32[]{:S(2)}, u32[]{:S(2)}) %collective-permute-start.3) | collective-permute-done | bytes 458784 | tf_op jit(solution)/shard_map/ppermute | solution.py:151
  60.9 1.8 collective-permute-start.5
  62.6 22.0 %collective-permute-done.4.refs_4_ = bf16[1,128,1792]{2,1,0:T(8,128)(2,1)S(1)} collective-permute-done((bf16[1,128,1792]{2,1,0:T(8,128)(2,1)}, bf16[1,128,1792]{2,1,0:T(8,128)(2,1)S(1)}, u32[]{:S(2)}, u32[]{:S(2)}) %collective-permute-start.4) | collective-permute-done | bytes 458784 | tf_op jit(solution)/shard_map/ppermute | solution.py:151
  84.7 4.7 %collective-permute-done.5.refs_5_ = bf16[1,128,1792]{2,1,0:T(8,128)(2,1)S(1)} collective-permute-done((bf16[1,128,1792]{2,1,0:T(8,128)(2,1)}, bf16[1,128,1792]{2,1,0:T(8,128)(2,1)S(1)}, u32[]{:S(2)}, u32[]{:S(2)}) %collective-permute-start.5) | collective-permute-done | bytes 458784 | tf_op jit(solution)/shard_map/ppermute | solution.py:151
  91.0 4.3 %shard_map.94 = (f32[3,32,1792]{2,1,0:T(8,128)}, bf16[3,32,1792]{2,1,0:T(8,128)(2,1)}, bf16[3,32,1792]{2,1,0:T(8,128)(2,1)}, bf16[3,32,1792]{2,1,0:T(8,128)(2,1)}) custom-call(f32[2,128,1792]{2,1,0:T(8,128)} %get-tuple-element.28.keep_gu, f32[1,128,1792]{2,1,0:T(8,128)} %get-tuple-element.30.keep_h, bf16[2,128,1792]{2,1,0:T(8,128)(2,1)} %copy-done.9, ...), custom_call_target="tpu_custom_call" | custom-call | tf_op jit(solution)/shard_map/pallas_call | solution.py:45
  95.3 1.6 collective-permute-start.6
  96.9 2.9 %collective-permute-start.7 = (bf16[3,32,1792]{2,1,0:T(8,128)(2,1)}, bf16[3,32,1792]{2,1,0:T(8,128)(2,1)S(1)}, u32[]{:S(2)}, u32[]{:S(2)}) collective-permute-start(bf16[3,32,1792]{2,1,0:T(8,128)(2,1)} %get-tuple-element.39), channel_id=1, source_target_pairs={{0,128},{1,33},{2,130},{3,35},{4,132},{5,37},{6,134},{7,39},{8,136... | collective-permute-start | bytes 1032200 | tf_op jit(solution)/shard_map/ppermute | solution.py:151
  99.8 1.3 collective-permute-start.8
  101.2 2.8 %collective-permute-done.6.got1 = bf16[3,32,1792]{2,1,0:T(8,128)(2,1)S(1)} collective-permute-done((bf16[3,32,1792]{2,1,0:T(8,128)(2,1)}, bf16[3,32,1792]{2,1,0:T(8,128)(2,1)S(1)}, u32[]{:S(2)}, u32[]{:S(2)}) %collective-permute-start.6) | collective-permute-done | bytes 344096 | tf_op jit(solution)/shard_map/ppermute | solution.py:151
  104.0 4.9 %collective-permute-done.7.got2 = bf16[3,32,1792]{2,1,0:T(8,128)(2,1)S(1)} collective-permute-done((bf16[3,32,1792]{2,1,0:T(8,128)(2,1)}, bf16[3,32,1792]{2,1,0:T(8,128)(2,1)S(1)}, u32[]{:S(2)}, u32[]{:S(2)}) %collective-permute-start.7) | collective-permute-done | bytes 344096 | tf_op jit(solution)/shard_map/ppermute | solution.py:151
  109.8 2.4 %shard_map.95.refs_0_ = bf16[3,32,1792]{2,1,0:T(8,128)(2,1)} custom-call(f32[3,32,1792]{2,1,0:T(8,128)} %get-tuple-element.37.own, bf16[3,32,1792]{2,1,0:T(8,128)(2,1)} %copy-done.20, bf16[3,32,1792]{2,1,0:T(8,128)(2,1)} %copy-done.21, bf16[3,32,1792]{2,1,0:T(8,128)(2,1)} %copy-done.22), custom_call_target="tpu_custom_call" | custom-call | tf_op jit(solution)/shard_map/pallas_call | solution.py:45
  112.2 2.2 %collective-permute-start.12 = (bf16[3,32,1792]{2,1,0:T(8,128)(2,1)}, bf16[3,32,1792]{2,1,0:T(8,128)(2,1)S(1)}, u32[]{:S(2)}, u32[]{:S(2)}) collective-permute-start(bf16[3,32,1792]{2,1,0:T(8,128)(2,1)} %shard_map.95.refs_0_), channel_id=1, source_target_pairs={{0,192},{1,49},{2,194},{3,51},{4,196},{5,53},{6,198},{7,55},{8,200... | collective-permute-start | bytes 1032200 | tf_op jit(solution)/shard_map/ppermute | solution.py:151
  114.3 1.4 collective-permute-start.13
  116.4 2.1 %collective-permute-start.10 = (bf16[3,32,1792]{2,1,0:T(8,128)(2,1)}, bf16[3,32,1792]{2,1,0:T(8,128)(2,1)S(1)}, u32[]{:S(2)}, u32[]{:S(2)}) collective-permute-start(bf16[3,32,1792]{2,1,0:T(8,128)(2,1)} %shard_map.95.refs_0_), channel_id=1, source_target_pairs={{0,32},{1,129},{2,34},{3,131},{4,36},{5,133},{6,38},{7,135},{8,40}... | collective-permute-start | bytes 1032200 | tf_op jit(solution)/shard_map/ppermute | solution.py:151
  118.5 11.6 %collective-permute-done.12.refs_0_ = bf16[3,32,1792]{2,1,0:T(8,128)(2,1)S(1)} collective-permute-done((bf16[3,32,1792]{2,1,0:T(8,128)(2,1)}, bf16[3,32,1792]{2,1,0:T(8,128)(2,1)S(1)}, u32[]{:S(2)}, u32[]{:S(2)}) %collective-permute-start.12) | collective-permute-done | bytes 344096 | tf_op jit(solution)/shard_map/ppermute | solution.py:151
  130.1 1.0 collective-permute-start.11
  131.1 3.2 %collective-permute-done.14.refs_2_ = bf16[3,32,1792]{2,1,0:T(8,128)(2,1)S(1)} collective-permute-done((bf16[3,32,1792]{2,1,0:T(8,128)(2,1)}, bf16[3,32,1792]{2,1,0:T(8,128)(2,1)S(1)}, u32[]{:S(2)}, u32[]{:S(2)}) %collective-permute-start.14) | collective-permute-done | bytes 344096 | tf_op jit(solution)/shard_map/ppermute | solution.py:151
  134.3 0.7 copy-done.19
  135.0 2.2 %shard_map.96 = (bf16[1,96,1792]{2,1,0:T(8,128)(2,1)}, bf16[2,96,1792]{2,1,0:T(8,128)(2,1)}) custom-call(bf16[3,32,1792]{2,1,0:T(8,128)(2,1)} %copy-done.17, bf16[3,32,1792]{2,1,0:T(8,128)(2,1)} %copy-done.18, bf16[3,32,1792]{2,1,0:T(8,128)(2,1)} %copy-done.19), custom_call_target="tpu_custom_call" | custom-call | tf_op jit(solution)/shard_map/pallas_call | solution.py:45
  137.3 2.2 %collective-permute-start.16 = (bf16[1,96,1792]{2,1,0:T(8,128)(2,1)}, bf16[1,96,1792]{2,1,0:T(8,128)(2,1)S(1)}, u32[]{:S(2)}, u32[]{:S(2)}) collective-permute-start(bf16[1,96,1792]{2,1,0:T(8,128)(2,1)} %get-tuple-element.41.refs_4_), channel_id=1, source_target_pairs={{0,32},{1,129},{2,34},{3,131},{4,36},{5,133},{6,38},{7,135},{8,40}... | collective-permute-start | bytes 1032200 | tf_op jit(solution)/shard_map/ppermute | solution.py:151
  139.5 1.9 collective-permute-start.17
  141.5 2.0 collective-permute-start.20
  143.5 1.2 collective-permute-done.15.refs_5_
  144.7 1.4 collective-permute-start.21
  146.1 2.6 %collective-permute-done.16.refs_6_ = bf16[1,96,1792]{2,1,0:T(8,128)(2,1)S(1)} collective-permute-done((bf16[1,96,1792]{2,1,0:T(8,128)(2,1)}, bf16[1,96,1792]{2,1,0:T(8,128)(2,1)S(1)}, u32[]{:S(2)}, u32[]{:S(2)}) %collective-permute-start.16) | collective-permute-done | bytes 344096 | tf_op jit(solution)/shard_map/ppermute | solution.py:151
  148.7 1.8 collective-permute-done.17.refs_7_
  151.2 4.5 %shard_map.97 = (f32[256,512]{1,0:T(8,128)}, f32[256,512]{1,0:T(8,128)}) custom-call(s32[16]{0:T(128)} %get-tuple-element.49.place, bf16[3,32,1792]{2,1,0:T(8,128)(2,1)} %shard_map.95.refs_0_, bf16[3,32,1792]{2,1,0:T(8,128)(2,1)} %copy-done, bf16[3,32,1792]{2,1,0:T(8,128)(2,1)} %copy-done.1, bf16[3,32,1792]{2,1,0:T(8,128)(2,1)} %copy-done.2, ...), custom_call_target="tpu_custom_call" | custom-call | tf_op jit(solution)/shard_map/pallas_call | solution.py:45
  156.0 7.4 %collective-permute-done.20.refs_6_ = bf16[2,96,1792]{2,1,0:T(8,128)(2,1)S(1)} collective-permute-done((bf16[2,96,1792]{2,1,0:T(8,128)(2,1)}, bf16[2,96,1792]{2,1,0:T(8,128)(2,1)S(1)}, u32[]{:S(2)}, u32[]{:S(2)}) %collective-permute-start.20) | collective-permute-done | bytes 688160 | tf_op jit(solution)/shard_map/ppermute | solution.py:151
  163.4 1.9 collective-permute-done.21.refs_7_
  165.3 0.9 copy-done.5
  166.2 6.4 %shard_map.98 = (f32[256,512]{1,0:T(8,128)}, f32[256,512]{1,0:T(8,128)}) custom-call(s32[16]{0:T(128)} %get-tuple-element.49.place, bf16[3,32,1792]{2,1,0:T(8,128)(2,1)} %shard_map.95.refs_0_, bf16[3,32,1792]{2,1,0:T(8,128)(2,1)} %copy-done, bf16[3,32,1792]{2,1,0:T(8,128)(2,1)} %copy-done.1, bf16[3,32,1792]{2,1,0:T(8,128)(2,1)} %copy-done.2, ...), custom_call_target="tpu_custom_call" | custom-call | tf_op jit(solution)/shard_map/pallas_call | solution.py:45
  172.6 0.8 add_convert_fusion.1
  173.4 4.3 %all-to-all-start = ((bf16[8,32,512]{2,1,0:T(8,128)(2,1)}), bf16[8,32,512]{2,1,0:T(8,128)(2,1)S(1)}, u32[]{:S(2)}, u32[]{:S(2)}) async-start(bf16[8,32,512]{2,1,0:T(8,128)(2,1)} %bitcast), calls=%async_computation | async-start | bytes 524288 | tf_op jit(solution)/shard_map/all_to_all | solution.py:164
  177.7 0.8 add_convert_fusion
  178.4 11.7 %all-to-all-done = bf16[8,32,512]{2,1,0:T(8,128)(2,1)S(1)} async-done(((bf16[8,32,512]{2,1,0:T(8,128)(2,1)}), bf16[8,32,512]{2,1,0:T(8,128)(2,1)S(1)}, u32[]{:S(2)}, u32[]{:S(2)}) %all-to-all-start) | async-done | bytes 262176 | tf_op jit(solution)/shard_map/all_to_all | solution.py:164
  190.2 3.6 %all-to-all-start.1 = ((bf16[8,32,512]{2,1,0:T(8,128)(2,1)}), bf16[8,32,512]{2,1,0:T(8,128)(2,1)S(1)}, u32[]{:S(2)}, u32[]{:S(2)}) async-start(bf16[8,32,512]{2,1,0:T(8,128)(2,1)} %bitcast.1), calls=%async_computation.1 | async-start | bytes 524288 | tf_op jit(solution)/shard_map/all_to_all | solution.py:164
  193.8 4.3 %shard_map.100 = bf16[1792,512]{1,0:T(8,128)(2,1)} custom-call(s32[16]{0:T(128)} %get-tuple-element.50.order, bf16[512,512]{1,0:T(8,128)(2,1)} %all_gather.7.left.og, bf16[3,32,1792]{2,1,0:T(8,128)(2,1)} %shard_map.95.refs_0_, bf16[3,32,1792]{2,1,0:T(8,128)(2,1)} %copy-done, bf16[3,32,1792]{2,1,0:T(8,128)(2,1)} %copy-done.1, bf16[3,32,1792]{2,1,0:T(8,128)(2,1)} %copy-done.2, ...), custom_call_target="tpu_custom_call" | custom-call | tf_op jit(solution)/shard_map/pallas_call | solution.py:45
  198.1 5.6 %shard_map.99 = (bf16[512,1792]{1,0:T(8,128)(2,1)}, bf16[512,1792]{1,0:T(8,128)(2,1)}) custom-call(s32[16]{0:T(128)} %get-tuple-element.50.order, bf16[512,512]{1,0:T(8,128)(2,1)} %all_gather.6.left.x, bf16[3,32,1792]{2,1,0:T(8,128)(2,1)} %shard_map.95.refs_0_, bf16[3,32,1792]{2,1,0:T(8,128)(2,1)} %copy-done, bf16[3,32,1792]{2,1,0:T(8,128)(2,1)} %copy-done.1, ...), custom_call_target="tpu_custom_call" | custom-call | tf_op jit(solution)/shard_map/pallas_call | solution.py:45
  204.4 1.5 all-to-all-done.1
  (72 shorter events, 6.2 us)
Async XLA Ops:
  24.2 6.4 %copy-start.23 = (bf16[32,512]{1,0:T(8,128)(2,1)S(1)}, bf16[32,512]{1,0:T(8,128)(2,1)}, u32[]{:S(2)}) copy-start(bf16[32,512]{1,0:T(8,128)(2,1)} %param.9) | copy-start | bytes 98308
  30.6 23.1 %copy-start.26 = (bf16[2,128,1792]{2,1,0:T(8,128)(2,1)S(1)}, bf16[2,128,1792]{2,1,0:T(8,128)(2,1)}, u32[]{:S(2)}) copy-start(bf16[2,128,1792]{2,1,0:T(8,128)(2,1)} %get-tuple-element.31) | copy-start | bytes 2752516
  30.6 24.3 %copy-start.25 = (bf16[2,128,1792]{2,1,0:T(8,128)(2,1)S(1)}, bf16[2,128,1792]{2,1,0:T(8,128)(2,1)}, u32[]{:S(2)}) copy-start(bf16[2,128,1792]{2,1,0:T(8,128)(2,1)} %get-tuple-element.32) | copy-start | bytes 2752516
  30.6 25.7 %copy-start.24 = (bf16[2,128,1792]{2,1,0:T(8,128)(2,1)S(1)}, bf16[2,128,1792]{2,1,0:T(8,128)(2,1)}, u32[]{:S(2)}) copy-start(bf16[2,128,1792]{2,1,0:T(8,128)(2,1)} %get-tuple-element.33) | copy-start | bytes 2752516
  52.2 8.7 %collective-permute-start.3 = (bf16[1,128,1792]{2,1,0:T(8,128)(2,1)}, bf16[1,128,1792]{2,1,0:T(8,128)(2,1)S(1)}, u32[]{:S(2)}, u32[]{:S(2)}) collective-permute-start(bf16[1,128,1792]{2,1,0:T(8,128)(2,1)} %get-tuple-element.34), channel_id=1, source_target_pairs={{0,16},{1,65},{2,18},{3,67},{4,20},{5,69},{6,22},{7,71},{8,24},{9,... | collective-permute-start | bytes 1376264 | tf_op jit(solution)/shard_map/ppermute | solution.py:151
  53.7 35.7 %collective-permute-start = (bf16[2,128,1792]{2,1,0:T(8,128)(2,1)S(1)}, bf16[2,128,1792]{2,1,0:T(8,128)(2,1)S(1)}, u32[]{:S(2)}, u32[]{:S(2)}) collective-permute-start(bf16[2,128,1792]{2,1,0:T(8,128)(2,1)S(1)} %copy-done.26), channel_id=1, source_target_pairs={{0,16},{1,65},{2,18},{3,67},{4,20},{5,69},{6,22},{7,71},{8,24},{9,... | collective-permute-start | bytes 2752520 | tf_op jit(solution)/shard_map/ppermute | solution.py:151
  54.9 34.5 %collective-permute-start.1 = (bf16[2,128,1792]{2,1,0:T(8,128)(2,1)S(1)}, bf16[2,128,1792]{2,1,0:T(8,128)(2,1)S(1)}, u32[]{:S(2)}, u32[]{:S(2)}) collective-permute-start(bf16[2,128,1792]{2,1,0:T(8,128)(2,1)S(1)} %copy-done.25), channel_id=1, source_target_pairs={{0,32},{1,129},{2,34},{3,131},{4,36},{5,133},{6,38},{7,135},{8,40}... | collective-permute-start | bytes 2752520 | tf_op jit(solution)/shard_map/ppermute | solution.py:151
  56.3 33.1 %collective-permute-start.2 = (bf16[2,128,1792]{2,1,0:T(8,128)(2,1)S(1)}, bf16[2,128,1792]{2,1,0:T(8,128)(2,1)S(1)}, u32[]{:S(2)}, u32[]{:S(2)}) collective-permute-start(bf16[2,128,1792]{2,1,0:T(8,128)(2,1)S(1)} %copy-done.24), channel_id=1, source_target_pairs={{0,48},{1,193},{2,50},{3,195},{4,52},{5,197},{6,54},{7,199},{8,56}... | collective-permute-start | bytes 2752520 | tf_op jit(solution)/shard_map/ppermute | solution.py:151
  57.4 27.2 %collective-permute-start.4 = (bf16[1,128,1792]{2,1,0:T(8,128)(2,1)}, bf16[1,128,1792]{2,1,0:T(8,128)(2,1)S(1)}, u32[]{:S(2)}, u32[]{:S(2)}) collective-permute-start(bf16[1,128,1792]{2,1,0:T(8,128)(2,1)} %get-tuple-element.35), channel_id=1, source_target_pairs={{0,32},{1,129},{2,34},{3,131},{4,36},{5,133},{6,38},{7,135},{8,40}... | collective-permute-start | bytes 1376264 | tf_op jit(solution)/shard_map/ppermute | solution.py:151
  60.9 28.5 %copy-start.14 = (bf16[1,128,1792]{2,1,0:T(8,128)(2,1)}, bf16[1,128,1792]{2,1,0:T(8,128)(2,1)S(1)}, u32[]{:S(2)}) copy-start(bf16[1,128,1792]{2,1,0:T(8,128)(2,1)S(1)} %collective-permute-done.3.refs_3_) | copy-start | bytes 1376260
  60.9 28.5 %collective-permute-start.5 = (bf16[1,128,1792]{2,1,0:T(8,128)(2,1)}, bf16[1,128,1792]{2,1,0:T(8,128)(2,1)S(1)}, u32[]{:S(2)}, u32[]{:S(2)}) collective-permute-start(bf16[1,128,1792]{2,1,0:T(8,128)(2,1)} %get-tuple-element.36), channel_id=1, source_target_pairs={{0,48},{1,193},{2,50},{3,195},{4,52},{5,197},{6,54},{7,199},{8,56}... | collective-permute-start | bytes 1376264 | tf_op jit(solution)/shard_map/ppermute | solution.py:151
  84.7 4.7 %copy-start.15 = (bf16[1,128,1792]{2,1,0:T(8,128)(2,1)}, bf16[1,128,1792]{2,1,0:T(8,128)(2,1)S(1)}, u32[]{:S(2)}) copy-start(bf16[1,128,1792]{2,1,0:T(8,128)(2,1)S(1)} %collective-permute-done.4.refs_4_) | copy-start | bytes 1376260
  89.3 1.1 copy-start.9
  89.3 1.4 copy-start.10
  89.4 1.6 copy-start.11
  95.3 8.7 %collective-permute-start.6 = (bf16[3,32,1792]{2,1,0:T(8,128)(2,1)}, bf16[3,32,1792]{2,1,0:T(8,128)(2,1)S(1)}, u32[]{:S(2)}, u32[]{:S(2)}) collective-permute-start(bf16[3,32,1792]{2,1,0:T(8,128)(2,1)} %get-tuple-element.38), channel_id=1, source_target_pairs={{0,64},{1,17},{2,66},{3,19},{4,68},{5,21},{6,70},{7,23},{8,72},{9,... | collective-permute-start | bytes 1032200 | tf_op jit(solution)/shard_map/ppermute | solution.py:151
  96.9 12.0 %collective-permute-start.7 = (bf16[3,32,1792]{2,1,0:T(8,128)(2,1)}, bf16[3,32,1792]{2,1,0:T(8,128)(2,1)S(1)}, u32[]{:S(2)}, u32[]{:S(2)}) collective-permute-start(bf16[3,32,1792]{2,1,0:T(8,128)(2,1)} %get-tuple-element.39), channel_id=1, source_target_pairs={{0,128},{1,33},{2,130},{3,35},{4,132},{5,37},{6,134},{7,39},{8,136... | collective-permute-start | bytes 1032200 | tf_op jit(solution)/shard_map/ppermute | solution.py:151
  99.8 9.1 %collective-permute-start.8 = (bf16[3,32,1792]{2,1,0:T(8,128)(2,1)}, bf16[3,32,1792]{2,1,0:T(8,128)(2,1)S(1)}, u32[]{:S(2)}, u32[]{:S(2)}) collective-permute-start(bf16[3,32,1792]{2,1,0:T(8,128)(2,1)} %get-tuple-element.40), channel_id=1, source_target_pairs={{0,192},{1,49},{2,194},{3,51},{4,196},{5,53},{6,198},{7,55},{8,200... | collective-permute-start | bytes 1032200 | tf_op jit(solution)/shard_map/ppermute | solution.py:151
  104.0 4.9 %copy-start.20 = (bf16[3,32,1792]{2,1,0:T(8,128)(2,1)}, bf16[3,32,1792]{2,1,0:T(8,128)(2,1)S(1)}, u32[]{:S(2)}) copy-start(bf16[3,32,1792]{2,1,0:T(8,128)(2,1)S(1)} %collective-permute-done.6.got1) | copy-start | bytes 1032196
  108.9 0.8 copy-start.22
  112.2 18.0 %collective-permute-start.12 = (bf16[3,32,1792]{2,1,0:T(8,128)(2,1)}, bf16[3,32,1792]{2,1,0:T(8,128)(2,1)S(1)}, u32[]{:S(2)}, u32[]{:S(2)}) collective-permute-start(bf16[3,32,1792]{2,1,0:T(8,128)(2,1)} %shard_map.95.refs_0_), channel_id=1, source_target_pairs={{0,192},{1,49},{2,194},{3,51},{4,196},{5,53},{6,198},{7,55},{8,200... | collective-permute-start | bytes 1032200 | tf_op jit(solution)/shard_map/ppermute | solution.py:151
  114.3 16.8 %collective-permute-start.13 = (bf16[3,32,1792]{2,1,0:T(8,128)(2,1)}, bf16[3,32,1792]{2,1,0:T(8,128)(2,1)S(1)}, u32[]{:S(2)}, u32[]{:S(2)}) collective-permute-start(bf16[3,32,1792]{2,1,0:T(8,128)(2,1)} %shard_map.95.refs_0_), channel_id=1, source_target_pairs={{0,128},{1,33},{2,130},{3,35},{4,132},{5,37},{6,134},{7,39},{8,136... | collective-permute-start | bytes 1032200 | tf_op jit(solution)/shard_map/ppermute | solution.py:151
  115.8 18.6 %collective-permute-start.14 = (bf16[3,32,1792]{2,1,0:T(8,128)(2,1)}, bf16[3,32,1792]{2,1,0:T(8,128)(2,1)S(1)}, u32[]{:S(2)}, u32[]{:S(2)}) collective-permute-start(bf16[3,32,1792]{2,1,0:T(8,128)(2,1)} %shard_map.95.refs_0_), channel_id=1, source_target_pairs={{0,64},{1,17},{2,66},{3,19},{4,68},{5,21},{6,70},{7,23},{8,72},{9,... | collective-permute-start | bytes 1032200 | tf_op jit(solution)/shard_map/ppermute | solution.py:151
  116.3 23.1 %collective-permute-start.9 = (bf16[3,32,1792]{2,1,0:T(8,128)(2,1)}, bf16[3,32,1792]{2,1,0:T(8,128)(2,1)S(1)}, u32[]{:S(2)}, u32[]{:S(2)}) collective-permute-start(bf16[3,32,1792]{2,1,0:T(8,128)(2,1)} %shard_map.95.refs_0_), channel_id=1, source_target_pairs={{0,48},{1,193},{2,50},{3,195},{4,52},{5,197},{6,54},{7,199},{8,56}... | collective-permute-start | bytes 1032200 | tf_op jit(solution)/shard_map/ppermute | solution.py:151
  116.4 24.9 %collective-permute-start.10 = (bf16[3,32,1792]{2,1,0:T(8,128)(2,1)}, bf16[3,32,1792]{2,1,0:T(8,128)(2,1)S(1)}, u32[]{:S(2)}, u32[]{:S(2)}) collective-permute-start(bf16[3,32,1792]{2,1,0:T(8,128)(2,1)} %shard_map.95.refs_0_), channel_id=1, source_target_pairs={{0,32},{1,129},{2,34},{3,131},{4,36},{5,133},{6,38},{7,135},{8,40}... | collective-permute-start | bytes 1032200 | tf_op jit(solution)/shard_map/ppermute | solution.py:151
  130.1 4.2 %copy-start.17 = (bf16[3,32,1792]{2,1,0:T(8,128)(2,1)}, bf16[3,32,1792]{2,1,0:T(8,128)(2,1)S(1)}, u32[]{:S(2)}) copy-start(bf16[3,32,1792]{2,1,0:T(8,128)(2,1)S(1)} %collective-permute-done.12.refs_0_) | copy-start | bytes 1032196
  130.1 11.4 %collective-permute-start.11 = (bf16[3,32,1792]{2,1,0:T(8,128)(2,1)}, bf16[3,32,1792]{2,1,0:T(8,128)(2,1)S(1)}, u32[]{:S(2)}, u32[]{:S(2)}) collective-permute-start(bf16[3,32,1792]{2,1,0:T(8,128)(2,1)} %shard_map.95.refs_0_), channel_id=1, source_target_pairs={{0,16},{1,65},{2,18},{3,67},{4,20},{5,69},{6,22},{7,71},{8,24},{9,... | collective-permute-start | bytes 1032200 | tf_op jit(solution)/shard_map/ppermute | solution.py:151
  131.1 3.2 %copy-start.18 = (bf16[3,32,1792]{2,1,0:T(8,128)(2,1)}, bf16[3,32,1792]{2,1,0:T(8,128)(2,1)S(1)}, u32[]{:S(2)}) copy-start(bf16[3,32,1792]{2,1,0:T(8,128)(2,1)S(1)} %collective-permute-done.13.refs_1_) | copy-start | bytes 1032196
  137.3 7.5 %collective-permute-start.15 = (bf16[1,96,1792]{2,1,0:T(8,128)(2,1)}, bf16[1,96,1792]{2,1,0:T(8,128)(2,1)S(1)}, u32[]{:S(2)}, u32[]{:S(2)}) collective-permute-start(bf16[1,96,1792]{2,1,0:T(8,128)(2,1)} %get-tuple-element.41.refs_4_), channel_id=1, source_target_pairs={{0,48},{1,193},{2,50},{3,195},{4,52},{5,197},{6,54},{7,199},{8,56}... | collective-permute-start | bytes 1032200 | tf_op jit(solution)/shard_map/ppermute | solution.py:151
  137.3 11.4 %collective-permute-start.16 = (bf16[1,96,1792]{2,1,0:T(8,128)(2,1)}, bf16[1,96,1792]{2,1,0:T(8,128)(2,1)S(1)}, u32[]{:S(2)}, u32[]{:S(2)}) collective-permute-start(bf16[1,96,1792]{2,1,0:T(8,128)(2,1)} %get-tuple-element.41.refs_4_), channel_id=1, source_target_pairs={{0,32},{1,129},{2,34},{3,131},{4,36},{5,133},{6,38},{7,135},{8,40}... | collective-permute-start | bytes 1032200 | tf_op jit(solution)/shard_map/ppermute | solution.py:151
  139.5 11.0 %copy-start = (bf16[3,32,1792]{2,1,0:T(8,128)(2,1)}, bf16[3,32,1792]{2,1,0:T(8,128)(2,1)S(1)}, u32[]{:S(2)}) copy-start(bf16[3,32,1792]{2,1,0:T(8,128)(2,1)S(1)} %collective-permute-done.9.refs_1_) | copy-start | bytes 1032196
  139.5 11.0 %collective-permute-start.17 = (bf16[1,96,1792]{2,1,0:T(8,128)(2,1)}, bf16[1,96,1792]{2,1,0:T(8,128)(2,1)S(1)}, u32[]{:S(2)}, u32[]{:S(2)}) collective-permute-start(bf16[1,96,1792]{2,1,0:T(8,128)(2,1)} %get-tuple-element.41.refs_4_), channel_id=1, source_target_pairs={{0,16},{1,65},{2,18},{3,67},{4,20},{5,69},{6,22},{7,71},{8,24},{9,... | collective-permute-start | bytes 1032200 | tf_op jit(solution)/shard_map/ppermute | solution.py:151
  141.3 9.2 %copy-start.1 = (bf16[3,32,1792]{2,1,0:T(8,128)(2,1)}, bf16[3,32,1792]{2,1,0:T(8,128)(2,1)S(1)}, u32[]{:S(2)}) copy-start(bf16[3,32,1792]{2,1,0:T(8,128)(2,1)S(1)} %collective-permute-done.10.refs_2_) | copy-start | bytes 1032196
  141.3 14.6 %collective-permute-start.19 = (bf16[2,96,1792]{2,1,0:T(8,128)(2,1)}, bf16[2,96,1792]{2,1,0:T(8,128)(2,1)S(1)}, u32[]{:S(2)}, u32[]{:S(2)}) collective-permute-start(bf16[2,96,1792]{2,1,0:T(8,128)(2,1)} %get-tuple-element.44.refs_4_), channel_id=1, source_target_pairs={{0,48},{1,193},{2,50},{3,195},{4,52},{5,197},{6,54},{7,199},{8,56}... | collective-permute-start | bytes 2064392 | tf_op jit(solution)/shard_map/ppermute | solution.py:151
  141.5 9.0 %copy-start.2 = (bf16[3,32,1792]{2,1,0:T(8,128)(2,1)}, bf16[3,32,1792]{2,1,0:T(8,128)(2,1)S(1)}, u32[]{:S(2)}) copy-start(bf16[3,32,1792]{2,1,0:T(8,128)(2,1)S(1)} %collective-permute-done.11.refs_3_) | copy-start | bytes 1032196
  141.5 21.9 %collective-permute-start.20 = (bf16[2,96,1792]{2,1,0:T(8,128)(2,1)}, bf16[2,96,1792]{2,1,0:T(8,128)(2,1)S(1)}, u32[]{:S(2)}, u32[]{:S(2)}) collective-permute-start(bf16[2,96,1792]{2,1,0:T(8,128)(2,1)} %get-tuple-element.44.refs_4_), channel_id=1, source_target_pairs={{0,32},{1,129},{2,34},{3,131},{4,36},{5,133},{6,38},{7,135},{8,40}... | collective-permute-start | bytes 2064392 | tf_op jit(solution)/shard_map/ppermute | solution.py:151
  144.7 5.8 %copy-start.6 = (bf16[1,96,1792]{2,1,0:T(8,128)(2,1)}, bf16[1,96,1792]{2,1,0:T(8,128)(2,1)S(1)}, u32[]{:S(2)}) copy-start(bf16[1,96,1792]{2,1,0:T(8,128)(2,1)S(1)} %collective-permute-done.15.refs_5_) | copy-start | bytes 1032196
  144.7 20.6 %collective-permute-start.21 = (bf16[2,96,1792]{2,1,0:T(8,128)(2,1)}, bf16[2,96,1792]{2,1,0:T(8,128)(2,1)S(1)}, u32[]{:S(2)}, u32[]{:S(2)}) collective-permute-start(bf16[2,96,1792]{2,1,0:T(8,128)(2,1)} %get-tuple-element.44.refs_4_), channel_id=1, source_target_pairs={{0,16},{1,65},{2,18},{3,67},{4,20},{5,69},{6,22},{7,71},{8,24},{9,... | collective-permute-start | bytes 2064392 | tf_op jit(solution)/shard_map/ppermute | solution.py:151
  148.7 1.8 copy-start.7
  155.7 16.9 %copy-start.12 = (f32[256,512]{1,0:T(8,128)S(1)}, f32[256,512]{1,0:T(8,128)}, u32[]{:S(2)}) copy-start(f32[256,512]{1,0:T(8,128)} %get-tuple-element.42) | copy-start | bytes 1572868
  155.7 16.9 %collective-permute-start.18 = (f32[256,512]{1,0:T(8,128)}, f32[256,512]{1,0:T(8,128)S(1)}, u32[]{:S(2)}, u32[]{:S(2)}) collective-permute-start(f32[256,512]{1,0:T(8,128)} %get-tuple-element.43), channel_id=1, source_target_pairs={{0,1},{1,0},{2,3},{3,2},{4,5},{5,4},{6,7},{7,6},{8,9},{9,8},{10,11... | collective-permute-start | bytes 1572872 | tf_op jit(solution)/shard_map/ppermute | solution.py:163
  156.0 9.3 %copy-start.3 = (bf16[2,96,1792]{2,1,0:T(8,128)(2,1)}, bf16[2,96,1792]{2,1,0:T(8,128)(2,1)S(1)}, u32[]{:S(2)}) copy-start(bf16[2,96,1792]{2,1,0:T(8,128)(2,1)S(1)} %collective-permute-done.19.refs_5_) | copy-start | bytes 2064388
  163.4 1.9 copy-start.4
  165.3 0.9 copy-start.5
  172.6 5.1 %copy-start.13 = (f32[256,512]{1,0:T(8,128)S(1)}, f32[256,512]{1,0:T(8,128)}, u32[]{:S(2)}) copy-start(f32[256,512]{1,0:T(8,128)} %get-tuple-element.45) | copy-start | bytes 1572868
  172.6 5.1 %collective-permute-start.22 = (f32[256,512]{1,0:T(8,128)}, f32[256,512]{1,0:T(8,128)S(1)}, u32[]{:S(2)}, u32[]{:S(2)}) collective-permute-start(f32[256,512]{1,0:T(8,128)} %get-tuple-element.46), channel_id=1, source_target_pairs={{0,1},{1,0},{2,3},{3,2},{4,5},{5,4},{6,7},{7,6},{8,9},{9,8},{10,11... | collective-permute-start | bytes 1572872 | tf_op jit(solution)/shard_map/ppermute | solution.py:163
  173.4 16.8 %all-to-all-start = ((bf16[8,32,512]{2,1,0:T(8,128)(2,1)}), bf16[8,32,512]{2,1,0:T(8,128)(2,1)S(1)}, u32[]{:S(2)}, u32[]{:S(2)}) async-start(bf16[8,32,512]{2,1,0:T(8,128)(2,1)} %bitcast), calls=%async_computation | async-start | bytes 524288 | tf_op jit(solution)/shard_map/all_to_all | solution.py:164
  190.2 15.7 %all-to-all-start.1 = ((bf16[8,32,512]{2,1,0:T(8,128)(2,1)}), bf16[8,32,512]{2,1,0:T(8,128)(2,1)S(1)}, u32[]{:S(2)}, u32[]{:S(2)}) async-start(bf16[8,32,512]{2,1,0:T(8,128)(2,1)} %bitcast.1), calls=%async_computation.1 | async-start | bytes 524288 | tf_op jit(solution)/shard_map/all_to_all | solution.py:164
  (4 other events, 3.0 us)

commit v2 on v1

v2 whole, which is shorter than its diff:
```python
import functools

import jax
import jax.numpy as jnp
from jax import lax
from jax.experimental import pallas as pl
from jax.experimental.pallas import tpu as pltpu
from jax.sharding import PartitionSpec as P


BF16, F32 = jnp.bfloat16, jnp.float32
SIDE = 4
DEEP = 8
BLOCKS = 16
VMEM_LIMIT = 56 * 1024 * 1024


def contract(left, right, left_dim, right_dim):
    return lax.dot_general(
        left, right, (((left_dim,), (right_dim,)), ((), ())), preferred_element_type=F32
    )


def shift(k, along):
    pairs = []
    for y in range(SIDE):
        for x in range(SIDE):
            for c in range(2 * DEEP):
                dy, dx = along if c % 2 == 0 else along[::-1]
                row = (y + k * dy) % SIDE * SIDE + (x + k * dx) % SIDE
                pairs.append(((y * SIDE + x) * 2 * DEEP + c, row * 2 * DEEP + c))
    return pairs


MAJOR, MINOR = (0, 1), (1, 0)


def partner():
    return [(c, c ^ 1) for c in range(2 * DEEP)]


def call(kernel, outs, n_scalar, args, scratch=(), blocks=None, steps=1):
    arrays = [(a.shape, a.dtype) for a in args[n_scalar:]] + list(outs)
    blocks = blocks or [None] * len(arrays)

    def spec(shape, cut):
        size = [d // steps if n == cut else d for n, d in enumerate(shape)]
        return pl.BlockSpec(tuple(size), lambda i: tuple(i if n == cut else 0 for n in range(len(shape))))

    specs = [spec(shape, cut) for (shape, _), cut in zip(arrays, blocks)]
    n_in = len(args) - n_scalar
    return pl.pallas_call(
        kernel,
        grid=(steps,),
        out_shape=[jax.ShapeDtypeStruct(s, d) for s, d in outs],
        in_specs=[pl.BlockSpec(memory_space=pltpu.SMEM)] * n_scalar + specs[:n_in],
        out_specs=specs[n_in:],
        scratch_shapes=scratch,
        compiler_params=pltpu.CompilerParams(vmem_limit_bytes=VMEM_LIMIT),
    )(*args)


def take_blocks(order, source, target):
    rows = source.shape[0] // BLOCKS
    for s in range(BLOCKS):
        at = pl.ds(pl.multiple_of(order[s] * rows, rows), rows)
        target[s * rows : (s + 1) * rows] = source[at, :]


def partial_kernel(dim, order, left, *refs):
    *weights, keep, send1, send2, send3, mine = refs

    @pl.when(pl.program_id(0) == 0)
    def _():
        take_blocks(order, left, mine)

    group = keep.shape[1]
    for n, weight in enumerate(weights):
        value = contract(mine[...], weight[...], 1, dim)
        keep[n] = value[:group]
        for k, send in enumerate((send1, send2, send3)):
            send[n] = value[(k + 1) * group : (k + 2) * group].astype(BF16)


def first_sum_kernel(keep, got1, got2, got3, *outs):
    rows = outs[0].shape[1]
    for k, out in enumerate(outs):
        at = slice(k * rows, (k + 1) * rows)
        total = keep[:, at, :]
        for got in (got1, got2, got3):
            total = total + got[:, at, :].astype(F32)
        out[...] = total.astype(out.dtype)


def last_sum(n, own, *gots):
    return own[n] + sum(got[n].astype(F32) for got in gots)


def hidden_kernel(*refs):
    sums, (hidden, factors) = refs[:SIDE], refs[SIDE:]
    gate, up = last_sum(0, *sums), last_sum(1, *sums)
    sig = jax.nn.sigmoid(gate)
    hidden[0] = (gate * sig * up).astype(BF16)
    factors[0] = up * (sig * (1.0 + gate * (1.0 - sig)))
    factors[1] = gate * sig


def parts_kernel(factors, *refs):
    sums, (parts,) = refs[:SIDE], refs[SIDE:]
    grad = last_sum(0, *sums)
    for n in range(2):
        parts[n] = (grad * factors[n]).astype(BF16)


def join_kernel(*refs):
    blocks, (out,) = refs[:SIDE], refs[SIDE:]
    rows = blocks[0].shape[1]
    for k, block in enumerate(blocks):
        out[:, k * rows : (k + 1) * rows, :] = block[...]


def stack_rows(pieces, n, target):
    rows = pieces[0].shape[1]
    for k, piece in enumerate(pieces):
        target[k * rows : (k + 1) * rows] = piece[n]


def product_kernel(dim, place, *refs):
    pieces, weights = refs[:SIDE], refs[SIDE:-4]
    mine, theirs, total, stack = refs[-4:]
    tokens = stack.shape[0]
    rows = tokens // BLOCKS
    step = pl.program_id(0)
    value = None
    for n, weight in enumerate(weights):
        stack_rows(pieces, n, stack)
        term = contract(stack[...], weight[...], 1, dim)
        value = term if value is None else value + term

    @pl.when(step == 0)
    def _():
        total[...] = value

    @pl.when(step == 1)
    def _():
        for s in range(BLOCKS):
            to = place[s]
            done = total[s * rows : (s + 1) * rows] + value[s * rows : (s + 1) * rows]

            @pl.when(to < DEEP)
            def _():
                mine[pl.ds(pl.multiple_of(to * rows, rows), rows), :] = done

            @pl.when(to >= DEEP)
            def _():
                theirs[pl.ds(pl.multiple_of((to - DEEP) * rows, rows), rows), :] = done


def down_grad_kernel(order, og, *refs):
    pieces, (down_grad, mine, stack) = refs[:SIDE], refs[SIDE:]
    take_blocks(order, og, mine)
    stack_rows(pieces, 0, stack)
    down_grad[...] = contract(stack[...], mine[...], 0, 0).astype(BF16)


def weight_grads_kernel(order, x, *refs):
    pieces, (gate_grad, up_grad, mine, stack) = refs[:SIDE], refs[SIDE:]
    take_blocks(order, x, mine)
    for n, grad in enumerate((gate_grad, up_grad)):
        stack_rows(pieces, n, stack)
        grad[...] = contract(mine[...], stack[...], 0, 0).astype(BF16)


def send(value, k, along):
    return lax.ppermute(value, ("row", "col"), shift(k, along))


def spread(values, along):
    return [send(v, k + 1, along) for k, v in enumerate(values)]


def collect(value, along):
    return [value] + [send(value, -k, along) for k in range(1, SIDE)]


def z_reduce(mine, theirs, wire, same_core):
    total = (mine + lax.ppermute(theirs, "col", partner())).astype(wire)
    got = lax.all_to_all(total, "col", 0, 0, axis_index_groups=same_core, tiled=True)
    return jnp.sum(got.reshape(DEEP, -1, got.shape[1]).astype(F32), axis=0).astype(BF16)


def on_device(inputs, gate_weight, up_weight, down_weight, out_grad):
    deep, width = gate_weight.shape
    row, col = lax.axis_index("row"), lax.axis_index("col")
    y, x, core = row // SIDE, row % SIDE, col % 2
    slot = jnp.arange(BLOCKS, dtype=jnp.int32)
    outer, inner = slot // SIDE, slot % SIDE
    dy, dx = jnp.where(core == 0, inner, outer), jnp.where(core == 0, outer, inner)
    order = (y + dy) % SIDE * SIDE + (x + dx) % SIDE
    place = (order + core) % 2 * DEEP + order // 2
    same_core = [[2 * z + c for z in range(DEEP)] for c in range(2)]

    all_inputs = lax.all_gather(inputs, "col", axis=0, tiled=True)
    tokens = all_inputs.shape[0]
    rows = tokens // BLOCKS
    group = SIDE * rows

    def partials(left, weights, dim):
        n = len(weights)
        return call(
            functools.partial(partial_kernel, dim),
            [((n, group, width), F32)] + [((n, group, width), BF16)] * 3,
            1,
            (order, left, *weights),
            [pltpu.VMEM((tokens, deep), BF16)],
            [None] + [1 - dim] * n + [2] * 4,
            2,
        )

    def product(pieces, weights, dim):
        return call(
            functools.partial(product_kernel, dim),
            [((tokens // 2, deep), F32)] * 2,
            1,
            (place, *pieces, *weights),
            [pltpu.VMEM((tokens, deep), F32), pltpu.VMEM((tokens, width // 2), BF16)],
            [2] * 4 + [dim] * len(weights) + [None] * 2,
            2,
        )

    keep_gu, *sends = partials(all_inputs, (gate_weight, up_weight), 0)
    got_gu = spread(sends, MAJOR)
    out_grad, keep_gu = lax.optimization_barrier((out_grad, keep_gu))
    all_grads = lax.all_gather(out_grad, "col", axis=0, tiled=True)
    keep_h, *sends = partials(all_grads, (down_weight,), 1)
    got_h = spread(sends, MAJOR)

    def first_sum(keep, got):
        n = keep.shape[0]
        return call(
            first_sum_kernel,
            [((n, rows, width), F32)] + [((n, rows, width), BF16)] * 3,
            0,
            (keep, *got),
            blocks=[2] * 8,
            steps=2,
        )

    def join(blocks):
        n = blocks[0].shape[0]
        (out,) = call(join_kernel, [((n, group, width), BF16)], 0, blocks, blocks=[2] * 5, steps=2)
        return out

    own_gu, *sends = first_sum(keep_gu, got_gu)
    got_gu = spread(sends, MINOR)
    own_h, *sends = first_sum(keep_h, got_h)
    got_h = spread(sends, MINOR)
    hidden, factors = call(
        hidden_kernel,
        [((1, rows, width), BF16), ((2, rows, width), F32)],
        0,
        (own_gu, *got_gu),
        blocks=[2] * 6,
        steps=2,
    )
    blocks_hidden = collect(hidden, MINOR)
    (parts,) = call(
        parts_kernel,
        [((2, rows, width), BF16)],
        0,
        (factors, own_h, *got_h),
        blocks=[2] * 6,
        steps=2,
    )
    blocks_parts = collect(parts, MINOR)
    hiddens = collect(join(blocks_hidden), MAJOR)
    grads = collect(join(blocks_parts), MAJOR)

    scratch = [pltpu.VMEM((tokens, deep), BF16), pltpu.VMEM((tokens, width), BF16)]
    sums = product(hiddens, (down_weight,), 0)
    output = z_reduce(*sums, BF16, same_core)
    (down_grad,) = call(
        down_grad_kernel, [((width, deep), BF16)], 1,
        (order, all_grads, *hiddens), scratch,
    )
    sums = product(grads, (gate_weight, up_weight), 1)
    in_grad = z_reduce(*sums, BF16, same_core)
    gate_grad, up_grad = call(
        weight_grads_kernel, [((deep, width), BF16)] * 2, 1,
        (order, all_inputs, *grads), scratch,
    )
    return (output, in_grad, gate_grad, up_grad, down_grad)


def solution(mesh):
    in_specs = (P("col", "row"), P("row", "col"), P("row", "col"), P("col", "row"), P("col", "row"))
    out_specs = (
        P("col", "row"),
        P("col", "row"),
        P("row", "col"),
        P("row", "col"),
        P("col", "row"),
    )
    return jax.shard_map(
        on_device, mesh=mesh, in_specs=in_specs, out_specs=out_specs, check_vma=False
    )
```

time: 209 us -> 215 us (1.029)
  starting transfers between devices: 36.9 us -> 39.6 us
  Pallas kernels: 40.1 us -> 42.7 us
    pallas_call x9 -> x12, Pallas kernels: 40.1 us -> 42.7 us  [call(): pl.pallas_call(kernel, grid=(steps,), out_shape=[jax.ShapeDtypeStruct(s,...]
    ppermute x21 -> x24, starting transfers between devices: 29 us -> 31.5 us  [send(): return lax.ppermute(value, ('row', 'col'), shift(k, along))]
    unnamed x54 -> x56, local copies, waits for them, and re-layouts: 4.8 us -> 6.61 us
    ppermute x21 -> x24, waiting for transfers between devices: 66.7 us -> 65.3 us  [send(): return lax.ppermute(value, ('row', 'col'), shift(k, along))]
  transfers between devices with their start and end apart: 25 -> 28, of which waited for: 15 -> 14; matrix products, arithmetic and copies ran while one was open for 1% -> 1% of each run, Pallas kernels for 11% -> 16%
where the time goes in v2:
time: 215 us; the launch traced here: 212 us
  waiting for transfers between devices  79 us (37%)
  Pallas kernels  42.7 us (20%)
  blocking collectives  40.2 us (19%)
  starting transfers between devices  39.6 us (18%)
  local copies, waits for them, and re-layouts  6.61 us (3%)
  other arithmetic  3.4 us (2%)
    ppermute x24, waiting for transfers between devices, send(): return lax.ppermute(value, ('row', 'col'), shift(k, along))  65.3 us
    pallas_call x12, Pallas kernels, call(): pl.pallas_call(kernel, grid=(steps,), out_shape=[jax.ShapeDtypeStruct(s,...  42.7 us
    ppermute x24, starting transfers between devices, send(): return lax.ppermute(value, ('row', 'col'), shift(k, along))  31.5 us
    all_gather x1, blocking collectives, on_device(): all_inputs = lax.all_gather(inputs, 'col', axis=0, tiled=True)  23.1 us
    all_gather x1, blocking collectives, on_device(): all_grads = lax.all_gather(out_grad, 'col', axis=0, tiled=True)  17.1 us
    all_to_all x2, waiting for transfers between devices, z_reduce(): lax.all_to_all(total, 'col', 0, 0, axis_index_groups=same_core, tiled=True)  13.6 us
    all_to_all x2, starting transfers between devices, z_reduce(): lax.all_to_all(total, 'col', 0, 0, axis_index_groups=same_core, tiled=True)  8.06 us
    unnamed x56, local copies, waits for them, and re-layouts  6.61 us
  transfers between devices with their start and end apart: 28, of which 14 were waited for; matrix products, arithmetic and copies ran while one was open for 1% of the time, Pallas kernels for 16%

profile of v2, /device:TPU:2, one launch (start us, length us, event | category | flops | bytes accessed | tf_op | source)
XLA Modules:
  0.0 212.3 jit_solution(1320619094215426263)
XLA Ops:
  0.7 23.1 %all_gather.6.left.x = bf16[512,512]{1,0:T(8,128)(2,1)} all-gather(bf16[32,512]{1,0:T(8,128)(2,1)} %param.5), channel_id=1, replica_groups=mesh['row'=16,'col'=16] {'col'}, dimensions={0}, use_global_device_ids=true | all-gather | bytes 557056 | tf_op jit(solution)/shard_map/all_gather | solution.py:203
  24.2 5.5 %shard_map.92 = (f32[2,128,1792]{2,1,0:T(8,128)}, bf16[2,128,1792]{2,1,0:T(8,128)(2,1)}, bf16[2,128,1792]{2,1,0:T(8,128)(2,1)}, bf16[2,128,1792]{2,1,0:T(8,128)(2,1)}) custom-call(s32[16]{0:T(128)} %get-tuple-element.58.order, bf16[512,512]{1,0:T(8,128)(2,1)} %all_gather.6.left.x, bf16[512,1792]{1,0:T(8,128)(2,1)} %refs_4_.3, bf16[512,1792]{1,0:T(8,128)(2,1)} %refs_5_.1), custom_call_target="tpu_custom_call" | custom-call | tf_op jit(solution)/shard_map/pallas_call | solution.py:52
  29.8 1.5 collective-permute-start
  31.3 1.1 collective-permute-start.1
  32.4 2.2 %collective-permute-start.2 = (bf16[2,128,1792]{2,1,0:T(8,128)(2,1)}, bf16[2,128,1792]{2,1,0:T(8,128)(2,1)S(1)}, u32[]{:S(2)}, u32[]{:S(2)}) collective-permute-start(bf16[2,128,1792]{2,1,0:T(8,128)(2,1)} %get-tuple-element.35), channel_id=1, source_target_pairs={{0,48},{1,193},{2,50},{3,195},{4,52},{5,197},{6,54},{7,199},{8,56}... | collective-permute-start | bytes 2752520 | tf_op jit(solution)/shard_map/ppermute | solution.py:175
  34.5 8.8 %collective-permute-done.got1 = bf16[2,128,1792]{2,1,0:T(8,128)(2,1)S(1)} collective-permute-done((bf16[2,128,1792]{2,1,0:T(8,128)(2,1)}, bf16[2,128,1792]{2,1,0:T(8,128)(2,1)S(1)}, u32[]{:S(2)}, u32[]{:S(2)}) %collective-permute-start) | collective-permute-done | bytes 917536 | tf_op jit(solution)/shard_map/ppermute | solution.py:175
  43.4 3.1 %collective-permute-done.1.got2 = bf16[2,128,1792]{2,1,0:T(8,128)(2,1)S(1)} collective-permute-done((bf16[2,128,1792]{2,1,0:T(8,128)(2,1)}, bf16[2,128,1792]{2,1,0:T(8,128)(2,1)S(1)}, u32[]{:S(2)}, u32[]{:S(2)}) %collective-permute-start.1) | collective-permute-done | bytes 917536 | tf_op jit(solution)/shard_map/ppermute | solution.py:175
  46.5 9.3 %collective-permute-done.2.got3 = bf16[2,128,1792]{2,1,0:T(8,128)(2,1)S(1)} collective-permute-done((bf16[2,128,1792]{2,1,0:T(8,128)(2,1)}, bf16[2,128,1792]{2,1,0:T(8,128)(2,1)S(1)}, u32[]{:S(2)}, u32[]{:S(2)}) %collective-permute-start.2) | collective-permute-done | bytes 917536 | tf_op jit(solution)/shard_map/ppermute | solution.py:175
  55.8 1.0 copy-done.9
  56.8 3.2 %shard_map.93 = (f32[2,32,1792]{2,1,0:T(8,128)}, bf16[2,32,1792]{2,1,0:T(8,128)(2,1)}, bf16[2,32,1792]{2,1,0:T(8,128)(2,1)}, bf16[2,32,1792]{2,1,0:T(8,128)(2,1)}) custom-call(f32[2,128,1792]{2,1,0:T(8,128)} %get-tuple-element.32.keep, bf16[2,128,1792]{2,1,0:T(8,128)(2,1)} %copy-done.7, bf16[2,128,1792]{2,1,0:T(8,128)(2,1)} %copy-done.8, ...), custom_call_target="tpu_custom_call" | custom-call | tf_op jit(solution)/shard_map/pallas_call | solution.py:52
  60.0 1.6 collective-permute-start.3
  61.6 2.9 %collective-permute-start.4 = (bf16[2,32,1792]{2,1,0:T(8,128)(2,1)}, bf16[2,32,1792]{2,1,0:T(8,128)(2,1)S(1)}, u32[]{:S(2)}, u32[]{:S(2)}) collective-permute-start(bf16[2,32,1792]{2,1,0:T(8,128)(2,1)} %get-tuple-element.38), channel_id=1, source_target_pairs={{0,128},{1,33},{2,130},{3,35},{4,132},{5,37},{6,134},{7,39},{8,136... | collective-permute-start | bytes 688136 | tf_op jit(solution)/shard_map/ppermute | solution.py:175
  64.5 1.3 collective-permute-start.5
  65.9 17.1 %all_gather.7.left.og = bf16[512,512]{1,0:T(8,128)(2,1)} all-gather(bf16[32,512]{1,0:T(8,128)(2,1)S(1)} %copy-done.27), channel_id=1, replica_groups=mesh['row'=16,'col'=16] {'col'}, dimensions={0}, use_global_device_ids=true | all-gather | bytes 557056 | tf_op jit(solution)/shard_map/all_gather | solution.py:234
  83.0 3.8 %shard_map.97 = (f32[1,128,1792]{2,1,0:T(8,128)}, bf16[1,128,1792]{2,1,0:T(8,128)(2,1)}, bf16[1,128,1792]{2,1,0:T(8,128)(2,1)}, bf16[1,128,1792]{2,1,0:T(8,128)(2,1)}) custom-call(s32[16]{0:T(128)} %get-tuple-element.58.order, bf16[512,512]{1,0:T(8,128)(2,1)} %all_gather.7.left.og, bf16[1792,512]{1,0:T(8,128)(2,1)} %refs_0_.3), custom_call_target="tpu_custom_call" | custom-call | tf_op jit(solution)/shard_map/pallas_call | solution.py:52
  86.8 1.0 collective-permute-start.13
  87.8 2.1 collective-permute-start.14
  89.9 1.0 collective-permute-start.15
  91.7 2.1 shard_map.94
  93.8 2.7 %collective-permute-start.7 = (bf16[1,32,1792]{2,1,0:T(8,128)(2,1)}, bf16[1,32,1792]{2,1,0:T(8,128)(2,1)S(1)}, u32[]{:S(2)}, u32[]{:S(2)}) collective-permute-start(bf16[1,32,1792]{2,1,0:T(8,128)(2,1)} %get-tuple-element.40.refs_0_), channel_id=1, source_target_pairs={{0,128},{1,33},{2,130},{3,35},{4,132},{5,37},{6,134},{7,39},{8,136... | collective-permute-start | bytes 344072 | tf_op jit(solution)/shard_map/ppermute | solution.py:175
  96.6 3.5 %collective-permute-done.6.refs_1_ = bf16[1,32,1792]{2,1,0:T(8,128)(2,1)S(1)} collective-permute-done((bf16[1,32,1792]{2,1,0:T(8,128)(2,1)}, bf16[1,32,1792]{2,1,0:T(8,128)(2,1)S(1)}, u32[]{:S(2)}, u32[]{:S(2)}) %collective-permute-start.6) | collective-permute-done | bytes 114720 | tf_op jit(solution)/shard_map/ppermute | solution.py:175
  100.7 5.5 %collective-permute-done.8.refs_3_ = bf16[1,32,1792]{2,1,0:T(8,128)(2,1)S(1)} collective-permute-done((bf16[1,32,1792]{2,1,0:T(8,128)(2,1)}, bf16[1,32,1792]{2,1,0:T(8,128)(2,1)S(1)}, u32[]{:S(2)}, u32[]{:S(2)}) %collective-permute-start.8) | collective-permute-done | bytes 114720 | tf_op jit(solution)/shard_map/ppermute | solution.py:175
  106.9 1.8 shard_map.95.refs_0_
  108.7 1.6 collective-permute-start.9
  111.3 2.4 %shard_map.98 = (f32[1,32,1792]{2,1,0:T(8,128)}, bf16[1,32,1792]{2,1,0:T(8,128)(2,1)}, bf16[1,32,1792]{2,1,0:T(8,128)(2,1)}, bf16[1,32,1792]{2,1,0:T(8,128)(2,1)}) custom-call(f32[1,128,1792]{2,1,0:T(8,128)} %get-tuple-element.45.keep, bf16[1,128,1792]{2,1,0:T(8,128)(2,1)} %copy-done.12, bf16[1,128,1792]{2,1,0:T(8,128)(2,1)} %copy-done.13, ...), custom_call_target="tpu_custom_call" | custom-call | tf_op jit(solution)/shard_map/pallas_call | solution.py:52
  114.0 1.5 collective-permute-start.17
  115.5 1.7 collective-permute-start.18
  117.2 4.2 %collective-permute-done.16.refs_1_ = bf16[1,32,1792]{2,1,0:T(8,128)(2,1)S(1)} collective-permute-done((bf16[1,32,1792]{2,1,0:T(8,128)(2,1)}, bf16[1,32,1792]{2,1,0:T(8,128)(2,1)S(1)}, u32[]{:S(2)}, u32[]{:S(2)}) %collective-permute-start.16) | collective-permute-done | bytes 114720 | tf_op jit(solution)/shard_map/ppermute | solution.py:175
  122.9 2.0 shard_map.99.refs_0_
  124.9 2.3 %collective-permute-start.19 = (bf16[2,32,1792]{2,1,0:T(8,128)(2,1)}, bf16[2,32,1792]{2,1,0:T(8,128)(2,1)S(1)}, u32[]{:S(2)}, u32[]{:S(2)}) collective-permute-start(bf16[2,32,1792]{2,1,0:T(8,128)(2,1)} %shard_map.99.refs_0_), channel_id=1, source_target_pairs={{0,192},{1,49},{2,194},{3,51},{4,196},{5,53},{6,198},{7,55},{8,200... | collective-permute-start | bytes 688136 | tf_op jit(solution)/shard_map/ppermute | solution.py:175
  128.1 0.9 collective-permute-start.10
  129.0 9.6 %collective-permute-done.19.refs_1_ = bf16[2,32,1792]{2,1,0:T(8,128)(2,1)S(1)} collective-permute-done((bf16[2,32,1792]{2,1,0:T(8,128)(2,1)}, bf16[2,32,1792]{2,1,0:T(8,128)(2,1)S(1)}, u32[]{:S(2)}, u32[]{:S(2)}) %collective-permute-start.19) | collective-permute-done | bytes 229408 | tf_op jit(solution)/shard_map/ppermute | solution.py:175
  139.0 4.0 %collective-permute-done.21.refs_3_ = bf16[2,32,1792]{2,1,0:T(8,128)(2,1)S(1)} collective-permute-done((bf16[2,32,1792]{2,1,0:T(8,128)(2,1)}, bf16[2,32,1792]{2,1,0:T(8,128)(2,1)S(1)}, u32[]{:S(2)}, u32[]{:S(2)}) %collective-permute-start.21) | collective-permute-done | bytes 229408 | tf_op jit(solution)/shard_map/ppermute | solution.py:175
  143.7 2.1 shard_map.100.refs_0_
  145.7 2.3 %collective-permute-start.23 = (bf16[2,128,1792]{2,1,0:T(8,128)(2,1)}, bf16[2,128,1792]{2,1,0:T(8,128)(2,1)S(1)}, u32[]{:S(2)}, u32[]{:S(2)}) collective-permute-start(bf16[2,128,1792]{2,1,0:T(8,128)(2,1)} %shard_map.100.refs_0_), channel_id=1, source_target_pairs={{0,32},{1,129},{2,34},{3,131},{4,36},{5,133},{6,38},{7,135},{8,40}... | collective-permute-start | bytes 2752520 | tf_op jit(solution)/shard_map/ppermute | solution.py:175
  148.1 1.5 collective-permute-start.24
  150.5 4.4 %shard_map.96 = (f32[256,512]{1,0:T(8,128)}, f32[256,512]{1,0:T(8,128)}) custom-call(s32[16]{0:T(128)} %get-tuple-element.57.place, bf16[1,128,1792]{2,1,0:T(8,128)(2,1)} %shard_map.95.refs_0_, bf16[1,128,1792]{2,1,0:T(8,128)(2,1)} %copy-done.4, bf16[1,128,1792]{2,1,0:T(8,128)(2,1)} %copy-done.5, bf16[1,128,1792]{2,1,0:T(8,128)(2,1)} %copy-done.6, ...), custom_call_target="tpu_custom_call" | custom-call | tf_op jit(solution)/shard_map/pallas_call | solution.py:52
  154.9 4.4 %collective-permute-done.22.refs_1_ = bf16[2,128,1792]{2,1,0:T(8,128)(2,1)S(1)} collective-permute-done((bf16[2,128,1792]{2,1,0:T(8,128)(2,1)}, bf16[2,128,1792]{2,1,0:T(8,128)(2,1)S(1)}, u32[]{:S(2)}, u32[]{:S(2)}) %collective-permute-start.22) | collective-permute-done | bytes 917536 | tf_op jit(solution)/shard_map/ppermute | solution.py:175
  159.3 10.1 %collective-permute-done.23.refs_2_ = bf16[2,128,1792]{2,1,0:T(8,128)(2,1)S(1)} collective-permute-done((bf16[2,128,1792]{2,1,0:T(8,128)(2,1)}, bf16[2,128,1792]{2,1,0:T(8,128)(2,1)S(1)}, u32[]{:S(2)}, u32[]{:S(2)}) %collective-permute-start.23) | collective-permute-done | bytes 917536 | tf_op jit(solution)/shard_map/ppermute | solution.py:175
  169.5 1.8 collective-permute-done.24.refs_3_
  171.3 0.9 copy-done.3
  172.2 6.0 %shard_map.101 = (f32[256,512]{1,0:T(8,128)}, f32[256,512]{1,0:T(8,128)}) custom-call(s32[16]{0:T(128)} %get-tuple-element.57.place, bf16[2,128,1792]{2,1,0:T(8,128)(2,1)} %shard_map.100.refs_0_, bf16[2,128,1792]{2,1,0:T(8,128)(2,1)} %copy-done.1, bf16[2,128,1792]{2,1,0:T(8,128)(2,1)} %copy-done.2, bf16[2,128,1792]{2,1,0:T(8,128)(2,1)} %copy-done.3, ...), custom_call_target="tpu_custom_call" | custom-call | tf_op jit(solution)/shard_map/pallas_call | solution.py:52
  179.0 4.4 %all-to-all-start = ((bf16[8,32,512]{2,1,0:T(8,128)(2,1)}), bf16[8,32,512]{2,1,0:T(8,128)(2,1)S(1)}, u32[]{:S(2)}, u32[]{:S(2)}) async-start(bf16[8,32,512]{2,1,0:T(8,128)(2,1)} %bitcast), calls=%async_computation | async-start | bytes 524288 | tf_op jit(solution)/shard_map/all_to_all | solution.py:188
  184.2 11.7 %all-to-all-done = bf16[8,32,512]{2,1,0:T(8,128)(2,1)S(1)} async-done(((bf16[8,32,512]{2,1,0:T(8,128)(2,1)}), bf16[8,32,512]{2,1,0:T(8,128)(2,1)S(1)}, u32[]{:S(2)}, u32[]{:S(2)}) %all-to-all-start) | async-done | bytes 262176 | tf_op jit(solution)/shard_map/all_to_all | solution.py:188
  196.0 3.6 %all-to-all-start.1 = ((bf16[8,32,512]{2,1,0:T(8,128)(2,1)}), bf16[8,32,512]{2,1,0:T(8,128)(2,1)S(1)}, u32[]{:S(2)}, u32[]{:S(2)}) async-start(bf16[8,32,512]{2,1,0:T(8,128)(2,1)} %bitcast.1), calls=%async_computation.1 | async-start | bytes 524288 | tf_op jit(solution)/shard_map/all_to_all | solution.py:188
  199.6 4.0 %shard_map.103 = bf16[1792,512]{1,0:T(8,128)(2,1)} custom-call(s32[16]{0:T(128)} %get-tuple-element.58.order, bf16[512,512]{1,0:T(8,128)(2,1)} %all_gather.7.left.og, bf16[1,128,1792]{2,1,0:T(8,128)(2,1)} %shard_map.95.refs_0_, bf16[1,128,1792]{2,1,0:T(8,128)(2,1)} %copy-done.4, bf16[1,128,1792]{2,1,0:T(8,128)(2,1)} %copy-done.5, bf16[1,128,1792]{2,1,0:T(8,128)(2,1)} %copy-done.6), custom_call_target="tpu_custom_call" | custom-call | tf_op jit(solution)/shard_map/pallas_call | solution.py:52
  203.6 5.5 %shard_map.102 = (bf16[512,1792]{1,0:T(8,128)(2,1)}, bf16[512,1792]{1,0:T(8,128)(2,1)}) custom-call(s32[16]{0:T(128)} %get-tuple-element.58.order, bf16[512,512]{1,0:T(8,128)(2,1)} %all_gather.6.left.x, bf16[2,128,1792]{2,1,0:T(8,128)(2,1)} %shard_map.100.refs_0_, bf16[2,128,1792]{2,1,0:T(8,128)(2,1)} %copy-done.1, bf16[2,128,1792]{2,1,0:T(8,128)(2,1)} %copy-done.2, ...), custom_call_target="tpu_custom_call" | custom-call | tf_op jit(solution)/shard_map/pallas_call | solution.py:52
  209.7 1.9 all-to-all-done.1
  (83 shorter events, 11.3 us)
Async XLA Ops:
  29.8 13.6 %collective-permute-start = (bf16[2,128,1792]{2,1,0:T(8,128)(2,1)}, bf16[2,128,1792]{2,1,0:T(8,128)(2,1)S(1)}, u32[]{:S(2)}, u32[]{:S(2)}) collective-permute-start(bf16[2,128,1792]{2,1,0:T(8,128)(2,1)} %get-tuple-element.33), channel_id=1, source_target_pairs={{0,16},{1,65},{2,18},{3,67},{4,20},{5,69},{6,22},{7,71},{8,24},{9,... | collective-permute-start | bytes 2752520 | tf_op jit(solution)/shard_map/ppermute | solution.py:175
  31.3 15.2 %collective-permute-start.1 = (bf16[2,128,1792]{2,1,0:T(8,128)(2,1)}, bf16[2,128,1792]{2,1,0:T(8,128)(2,1)S(1)}, u32[]{:S(2)}, u32[]{:S(2)}) collective-permute-start(bf16[2,128,1792]{2,1,0:T(8,128)(2,1)} %get-tuple-element.34), channel_id=1, source_target_pairs={{0,32},{1,129},{2,34},{3,131},{4,36},{5,133},{6,38},{7,135},{8,40}... | collective-permute-start | bytes 2752520 | tf_op jit(solution)/shard_map/ppermute | solution.py:175
  32.4 23.4 %collective-permute-start.2 = (bf16[2,128,1792]{2,1,0:T(8,128)(2,1)}, bf16[2,128,1792]{2,1,0:T(8,128)(2,1)S(1)}, u32[]{:S(2)}, u32[]{:S(2)}) collective-permute-start(bf16[2,128,1792]{2,1,0:T(8,128)(2,1)} %get-tuple-element.35), channel_id=1, source_target_pairs={{0,48},{1,193},{2,50},{3,195},{4,52},{5,197},{6,54},{7,199},{8,56}... | collective-permute-start | bytes 2752520 | tf_op jit(solution)/shard_map/ppermute | solution.py:175
  34.5 31.3 %copy-start.27 = (bf16[32,512]{1,0:T(8,128)(2,1)S(1)}, bf16[32,512]{1,0:T(8,128)(2,1)}, u32[]{:S(2)}) copy-start(bf16[32,512]{1,0:T(8,128)(2,1)} %param.9) | copy-start | bytes 98308
  43.4 12.4 %copy-start.7 = (bf16[2,128,1792]{2,1,0:T(8,128)(2,1)}, bf16[2,128,1792]{2,1,0:T(8,128)(2,1)S(1)}, u32[]{:S(2)}) copy-start(bf16[2,128,1792]{2,1,0:T(8,128)(2,1)S(1)} %collective-permute-done.got1) | copy-start | bytes 2752516
  46.5 9.3 %copy-start.8 = (bf16[2,128,1792]{2,1,0:T(8,128)(2,1)}, bf16[2,128,1792]{2,1,0:T(8,128)(2,1)S(1)}, u32[]{:S(2)}) copy-start(bf16[2,128,1792]{2,1,0:T(8,128)(2,1)S(1)} %collective-permute-done.1.got2) | copy-start | bytes 2752516
  55.8 1.0 copy-start.9
  60.0 29.9 %collective-permute-start.3 = (bf16[2,32,1792]{2,1,0:T(8,128)(2,1)}, bf16[2,32,1792]{2,1,0:T(8,128)(2,1)S(1)}, u32[]{:S(2)}, u32[]{:S(2)}) collective-permute-start(bf16[2,32,1792]{2,1,0:T(8,128)(2,1)} %get-tuple-element.37), channel_id=1, source_target_pairs={{0,64},{1,17},{2,66},{3,19},{4,68},{5,21},{6,70},{7,23},{8,72},{9,... | collective-permute-start | bytes 688136 | tf_op jit(solution)/shard_map/ppermute | solution.py:175
  61.6 29.3 %collective-permute-start.4 = (bf16[2,32,1792]{2,1,0:T(8,128)(2,1)}, bf16[2,32,1792]{2,1,0:T(8,128)(2,1)S(1)}, u32[]{:S(2)}, u32[]{:S(2)}) collective-permute-start(bf16[2,32,1792]{2,1,0:T(8,128)(2,1)} %get-tuple-element.38), channel_id=1, source_target_pairs={{0,128},{1,33},{2,130},{3,35},{4,132},{5,37},{6,134},{7,39},{8,136... | collective-permute-start | bytes 688136 | tf_op jit(solution)/shard_map/ppermute | solution.py:175
  64.5 26.4 %collective-permute-start.5 = (bf16[2,32,1792]{2,1,0:T(8,128)(2,1)}, bf16[2,32,1792]{2,1,0:T(8,128)(2,1)S(1)}, u32[]{:S(2)}, u32[]{:S(2)}) collective-permute-start(bf16[2,32,1792]{2,1,0:T(8,128)(2,1)} %get-tuple-element.39), channel_id=1, source_target_pairs={{0,192},{1,49},{2,194},{3,51},{4,196},{5,53},{6,198},{7,55},{8,200... | collective-permute-start | bytes 688136 | tf_op jit(solution)/shard_map/ppermute | solution.py:175
  86.8 23.5 %collective-permute-start.13 = (bf16[1,128,1792]{2,1,0:T(8,128)(2,1)}, bf16[1,128,1792]{2,1,0:T(8,128)(2,1)S(1)}, u32[]{:S(2)}, u32[]{:S(2)}) collective-permute-start(bf16[1,128,1792]{2,1,0:T(8,128)(2,1)} %get-tuple-element.46), channel_id=1, source_target_pairs={{0,16},{1,65},{2,18},{3,67},{4,20},{5,69},{6,22},{7,71},{8,24},{9,... | collective-permute-start | bytes 1376264 | tf_op jit(solution)/shard_map/ppermute | solution.py:175
  87.8 22.5 %collective-permute-start.14 = (bf16[1,128,1792]{2,1,0:T(8,128)(2,1)}, bf16[1,128,1792]{2,1,0:T(8,128)(2,1)S(1)}, u32[]{:S(2)}, u32[]{:S(2)}) collective-permute-start(bf16[1,128,1792]{2,1,0:T(8,128)(2,1)} %get-tuple-element.47), channel_id=1, source_target_pairs={{0,32},{1,129},{2,34},{3,131},{4,36},{5,133},{6,38},{7,135},{8,40}... | collective-permute-start | bytes 1376264 | tf_op jit(solution)/shard_map/ppermute | solution.py:175
  89.9 1.1 copy-start.18
  89.9 20.4 %collective-permute-start.15 = (bf16[1,128,1792]{2,1,0:T(8,128)(2,1)}, bf16[1,128,1792]{2,1,0:T(8,128)(2,1)S(1)}, u32[]{:S(2)}, u32[]{:S(2)}) collective-permute-start(bf16[1,128,1792]{2,1,0:T(8,128)(2,1)} %get-tuple-element.48), channel_id=1, source_target_pairs={{0,48},{1,193},{2,50},{3,195},{4,52},{5,197},{6,54},{7,199},{8,56}... | collective-permute-start | bytes 1376264 | tf_op jit(solution)/shard_map/ppermute | solution.py:175
  93.8 6.2 %collective-permute-start.6 = (bf16[1,32,1792]{2,1,0:T(8,128)(2,1)}, bf16[1,32,1792]{2,1,0:T(8,128)(2,1)S(1)}, u32[]{:S(2)}, u32[]{:S(2)}) collective-permute-start(bf16[1,32,1792]{2,1,0:T(8,128)(2,1)} %get-tuple-element.40.refs_0_), channel_id=1, source_target_pairs={{0,192},{1,49},{2,194},{3,51},{4,196},{5,53},{6,198},{7,55},{8,200... | collective-permute-start | bytes 344072 | tf_op jit(solution)/shard_map/ppermute | solution.py:175
  93.8 6.9 %collective-permute-start.7 = (bf16[1,32,1792]{2,1,0:T(8,128)(2,1)}, bf16[1,32,1792]{2,1,0:T(8,128)(2,1)S(1)}, u32[]{:S(2)}, u32[]{:S(2)}) collective-permute-start(bf16[1,32,1792]{2,1,0:T(8,128)(2,1)} %get-tuple-element.40.refs_0_), channel_id=1, source_target_pairs={{0,128},{1,33},{2,130},{3,35},{4,132},{5,37},{6,134},{7,39},{8,136... | collective-permute-start | bytes 344072 | tf_op jit(solution)/shard_map/ppermute | solution.py:175
  100.1 6.2 %copy-start.24 = (bf16[1,32,1792]{2,1,0:T(8,128)(2,1)}, bf16[1,32,1792]{2,1,0:T(8,128)(2,1)S(1)}, u32[]{:S(2)}) copy-start(bf16[1,32,1792]{2,1,0:T(8,128)(2,1)S(1)} %collective-permute-done.6.refs_1_) | copy-start | bytes 344068
  100.1 6.2 %collective-permute-start.8 = (bf16[1,32,1792]{2,1,0:T(8,128)(2,1)}, bf16[1,32,1792]{2,1,0:T(8,128)(2,1)S(1)}, u32[]{:S(2)}, u32[]{:S(2)}) collective-permute-start(bf16[1,32,1792]{2,1,0:T(8,128)(2,1)} %get-tuple-element.40.refs_0_), channel_id=1, source_target_pairs={{0,64},{1,17},{2,66},{3,19},{4,68},{5,21},{6,70},{7,23},{8,72},{9,... | collective-permute-start | bytes 344072 | tf_op jit(solution)/shard_map/ppermute | solution.py:175
  100.7 5.5 %copy-start.25 = (bf16[1,32,1792]{2,1,0:T(8,128)(2,1)}, bf16[1,32,1792]{2,1,0:T(8,128)(2,1)S(1)}, u32[]{:S(2)}) copy-start(bf16[1,32,1792]{2,1,0:T(8,128)(2,1)S(1)} %collective-permute-done.7.refs_2_) | copy-start | bytes 344068
  108.7 19.4 %copy-start = (bf16[1,128,1792]{2,1,0:T(8,128)(2,1)S(1)}, bf16[1,128,1792]{2,1,0:T(8,128)(2,1)}, u32[]{:S(2)}) copy-start(bf16[1,128,1792]{2,1,0:T(8,128)(2,1)} %shard_map.95.refs_0_) | copy-start | bytes 1376260
  108.7 39.4 %collective-permute-start.9 = (bf16[1,128,1792]{2,1,0:T(8,128)(2,1)}, bf16[1,128,1792]{2,1,0:T(8,128)(2,1)S(1)}, u32[]{:S(2)}, u32[]{:S(2)}) collective-permute-start(bf16[1,128,1792]{2,1,0:T(8,128)(2,1)} %shard_map.95.refs_0_), channel_id=1, source_target_pairs={{0,48},{1,193},{2,50},{3,195},{4,52},{5,197},{6,54},{7,199},{8,56}... | collective-permute-start | bytes 1376264 | tf_op jit(solution)/shard_map/ppermute | solution.py:175
  110.3 0.9 copy-start.13
  110.3 1.0 copy-start.14
  113.7 7.7 %collective-permute-start.16 = (bf16[1,32,1792]{2,1,0:T(8,128)(2,1)}, bf16[1,32,1792]{2,1,0:T(8,128)(2,1)S(1)}, u32[]{:S(2)}, u32[]{:S(2)}) collective-permute-start(bf16[1,32,1792]{2,1,0:T(8,128)(2,1)} %get-tuple-element.50), channel_id=1, source_target_pairs={{0,64},{1,17},{2,66},{3,19},{4,68},{5,21},{6,70},{7,23},{8,72},{9,... | collective-permute-start | bytes 344072 | tf_op jit(solution)/shard_map/ppermute | solution.py:175
  114.0 7.4 %collective-permute-start.17 = (bf16[1,32,1792]{2,1,0:T(8,128)(2,1)}, bf16[1,32,1792]{2,1,0:T(8,128)(2,1)S(1)}, u32[]{:S(2)}, u32[]{:S(2)}) collective-permute-start(bf16[1,32,1792]{2,1,0:T(8,128)(2,1)} %get-tuple-element.51), channel_id=1, source_target_pairs={{0,128},{1,33},{2,130},{3,35},{4,132},{5,37},{6,134},{7,39},{8,136... | collective-permute-start | bytes 344072 | tf_op jit(solution)/shard_map/ppermute | solution.py:175
  115.5 6.8 %collective-permute-start.18 = (bf16[1,32,1792]{2,1,0:T(8,128)(2,1)}, bf16[1,32,1792]{2,1,0:T(8,128)(2,1)S(1)}, u32[]{:S(2)}, u32[]{:S(2)}) collective-permute-start(bf16[1,32,1792]{2,1,0:T(8,128)(2,1)} %get-tuple-element.52), channel_id=1, source_target_pairs={{0,192},{1,49},{2,194},{3,51},{4,196},{5,53},{6,198},{7,55},{8,200... | collective-permute-start | bytes 344072 | tf_op jit(solution)/shard_map/ppermute | solution.py:175
  121.4 0.9 copy-start.21
  124.9 13.7 %collective-permute-start.19 = (bf16[2,32,1792]{2,1,0:T(8,128)(2,1)}, bf16[2,32,1792]{2,1,0:T(8,128)(2,1)S(1)}, u32[]{:S(2)}, u32[]{:S(2)}) collective-permute-start(bf16[2,32,1792]{2,1,0:T(8,128)(2,1)} %shard_map.99.refs_0_), channel_id=1, source_target_pairs={{0,192},{1,49},{2,194},{3,51},{4,196},{5,53},{6,198},{7,55},{8,200... | collective-permute-start | bytes 688136 | tf_op jit(solution)/shard_map/ppermute | solution.py:175
  127.2 11.7 %collective-permute-start.20 = (bf16[2,32,1792]{2,1,0:T(8,128)(2,1)}, bf16[2,32,1792]{2,1,0:T(8,128)(2,1)S(1)}, u32[]{:S(2)}, u32[]{:S(2)}) collective-permute-start(bf16[2,32,1792]{2,1,0:T(8,128)(2,1)} %shard_map.99.refs_0_), channel_id=1, source_target_pairs={{0,128},{1,33},{2,130},{3,35},{4,132},{5,37},{6,134},{7,39},{8,136... | collective-permute-start | bytes 688136 | tf_op jit(solution)/shard_map/ppermute | solution.py:175
  127.7 15.2 %collective-permute-start.21 = (bf16[2,32,1792]{2,1,0:T(8,128)(2,1)}, bf16[2,32,1792]{2,1,0:T(8,128)(2,1)S(1)}, u32[]{:S(2)}, u32[]{:S(2)}) collective-permute-start(bf16[2,32,1792]{2,1,0:T(8,128)(2,1)} %shard_map.99.refs_0_), channel_id=1, source_target_pairs={{0,64},{1,17},{2,66},{3,19},{4,68},{5,21},{6,70},{7,23},{8,72},{9,... | collective-permute-start | bytes 688136 | tf_op jit(solution)/shard_map/ppermute | solution.py:175
  128.1 21.5 %collective-permute-start.10 = (bf16[1,128,1792]{2,1,0:T(8,128)(2,1)S(1)}, bf16[1,128,1792]{2,1,0:T(8,128)(2,1)S(1)}, u32[]{:S(2)}, u32[]{:S(2)}) collective-permute-start(bf16[1,128,1792]{2,1,0:T(8,128)(2,1)S(1)} %copy-done), channel_id=1, source_target_pairs={{0,32},{1,129},{2,34},{3,131},{4,36},{5,133},{6,38},{7,135},{8,40}... | collective-permute-start | bytes 1376264 | tf_op jit(solution)/shard_map/ppermute | solution.py:175
  138.6 4.4 %copy-start.15 = (bf16[2,32,1792]{2,1,0:T(8,128)(2,1)}, bf16[2,32,1792]{2,1,0:T(8,128)(2,1)S(1)}, u32[]{:S(2)}) copy-start(bf16[2,32,1792]{2,1,0:T(8,128)(2,1)S(1)} %collective-permute-done.19.refs_1_) | copy-start | bytes 688132
  138.6 11.0 %collective-permute-start.11 = (bf16[1,128,1792]{2,1,0:T(8,128)(2,1)S(1)}, bf16[1,128,1792]{2,1,0:T(8,128)(2,1)S(1)}, u32[]{:S(2)}, u32[]{:S(2)}) collective-permute-start(bf16[1,128,1792]{2,1,0:T(8,128)(2,1)S(1)} %copy-done), channel_id=1, source_target_pairs={{0,16},{1,65},{2,18},{3,67},{4,20},{5,69},{6,22},{7,71},{8,24},{9,... | collective-permute-start | bytes 1376264 | tf_op jit(solution)/shard_map/ppermute | solution.py:175
  139.0 4.0 %copy-start.16 = (bf16[2,32,1792]{2,1,0:T(8,128)(2,1)}, bf16[2,32,1792]{2,1,0:T(8,128)(2,1)S(1)}, u32[]{:S(2)}) copy-start(bf16[2,32,1792]{2,1,0:T(8,128)(2,1)S(1)} %collective-permute-done.20.refs_2_) | copy-start | bytes 688132
  145.7 13.6 %collective-permute-start.22 = (bf16[2,128,1792]{2,1,0:T(8,128)(2,1)}, bf16[2,128,1792]{2,1,0:T(8,128)(2,1)S(1)}, u32[]{:S(2)}, u32[]{:S(2)}) collective-permute-start(bf16[2,128,1792]{2,1,0:T(8,128)(2,1)} %shard_map.100.refs_0_), channel_id=1, source_target_pairs={{0,48},{1,193},{2,50},{3,195},{4,52},{5,197},{6,54},{7,199},{8,56}... | collective-permute-start | bytes 2752520 | tf_op jit(solution)/shard_map/ppermute | solution.py:175
  145.7 23.7 %collective-permute-start.23 = (bf16[2,128,1792]{2,1,0:T(8,128)(2,1)}, bf16[2,128,1792]{2,1,0:T(8,128)(2,1)S(1)}, u32[]{:S(2)}, u32[]{:S(2)}) collective-permute-start(bf16[2,128,1792]{2,1,0:T(8,128)(2,1)} %shard_map.100.refs_0_), channel_id=1, source_target_pairs={{0,32},{1,129},{2,34},{3,131},{4,36},{5,133},{6,38},{7,135},{8,40}... | collective-permute-start | bytes 2752520 | tf_op jit(solution)/shard_map/ppermute | solution.py:175
  148.1 1.5 copy-start.4
  148.1 23.2 %collective-permute-start.24 = (bf16[2,128,1792]{2,1,0:T(8,128)(2,1)}, bf16[2,128,1792]{2,1,0:T(8,128)(2,1)S(1)}, u32[]{:S(2)}, u32[]{:S(2)}) collective-permute-start(bf16[2,128,1792]{2,1,0:T(8,128)(2,1)} %shard_map.100.refs_0_), channel_id=1, source_target_pairs={{0,16},{1,65},{2,18},{3,67},{4,20},{5,69},{6,22},{7,71},{8,24},{9,... | collective-permute-start | bytes 2752520 | tf_op jit(solution)/shard_map/ppermute | solution.py:175
  149.6 0.9 copy-start.6
  154.9 23.3 %copy-start.10 = (f32[256,512]{1,0:T(8,128)S(1)}, f32[256,512]{1,0:T(8,128)}, u32[]{:S(2)}) copy-start(f32[256,512]{1,0:T(8,128)} %get-tuple-element.41) | copy-start | bytes 1572868
  154.9 23.3 %collective-permute-start.12 = (f32[256,512]{1,0:T(8,128)}, f32[256,512]{1,0:T(8,128)S(1)}, u32[]{:S(2)}, u32[]{:S(2)}) collective-permute-start(f32[256,512]{1,0:T(8,128)} %get-tuple-element.42), channel_id=1, source_target_pairs={{0,1},{1,0},{2,3},{3,2},{4,5},{5,4},{6,7},{7,6},{8,9},{9,8},{10,11... | collective-permute-start | bytes 1572872 | tf_op jit(solution)/shard_map/ppermute | solution.py:187
  159.3 11.9 %copy-start.1 = (bf16[2,128,1792]{2,1,0:T(8,128)(2,1)}, bf16[2,128,1792]{2,1,0:T(8,128)(2,1)S(1)}, u32[]{:S(2)}) copy-start(bf16[2,128,1792]{2,1,0:T(8,128)(2,1)S(1)} %collective-permute-done.22.refs_1_) | copy-start | bytes 2752516
  169.5 1.8 copy-start.2
  171.3 0.9 copy-start.3
  178.2 5.3 %copy-start.11 = (f32[256,512]{1,0:T(8,128)S(1)}, f32[256,512]{1,0:T(8,128)}, u32[]{:S(2)}) copy-start(f32[256,512]{1,0:T(8,128)} %get-tuple-element.53) | copy-start | bytes 1572868
  178.2 5.3 %collective-permute-start.25 = (f32[256,512]{1,0:T(8,128)}, f32[256,512]{1,0:T(8,128)S(1)}, u32[]{:S(2)}, u32[]{:S(2)}) collective-permute-start(f32[256,512]{1,0:T(8,128)} %get-tuple-element.54), channel_id=1, source_target_pairs={{0,1},{1,0},{2,3},{3,2},{4,5},{5,4},{6,7},{7,6},{8,9},{9,8},{10,11... | collective-permute-start | bytes 1572872 | tf_op jit(solution)/shard_map/ppermute | solution.py:187
  179.0 17.0 %all-to-all-start = ((bf16[8,32,512]{2,1,0:T(8,128)(2,1)}), bf16[8,32,512]{2,1,0:T(8,128)(2,1)S(1)}, u32[]{:S(2)}, u32[]{:S(2)}) async-start(bf16[8,32,512]{2,1,0:T(8,128)(2,1)} %bitcast), calls=%async_computation | async-start | bytes 524288 | tf_op jit(solution)/shard_map/all_to_all | solution.py:188
  196.0 15.7 %all-to-all-start.1 = ((bf16[8,32,512]{2,1,0:T(8,128)(2,1)}), bf16[8,32,512]{2,1,0:T(8,128)(2,1)S(1)}, u32[]{:S(2)}, u32[]{:S(2)}) async-start(bf16[8,32,512]{2,1,0:T(8,128)(2,1)} %bitcast.1), calls=%async_computation.1 | async-start | bytes 524288 | tf_op jit(solution)/shard_map/all_to_all | solution.py:188
  (8 other events, 5.9 us)

commit v3 on v2

--- a/solution.py
+++ b/solution.py
@@ -12,7 +12,7 @@
 SIDE = 4
 DEEP = 8
 BLOCKS = 16
-VMEM_LIMIT = 56 * 1024 * 1024
+VMEM_LIMIT = 24 * 1024 * 1024
 
 
 def contract(left, right, left_dim, right_dim):
@@ -39,25 +39,19 @@
     return [(c, c ^ 1) for c in range(2 * DEEP)]
 
 
-def call(kernel, outs, n_scalar, args, scratch=(), blocks=None, steps=1):
-    arrays = [(a.shape, a.dtype) for a in args[n_scalar:]] + list(outs)
-    blocks = blocks or [None] * len(arrays)
-
-    def spec(shape, cut):
-        size = [d // steps if n == cut else d for n, d in enumerate(shape)]
-        return pl.BlockSpec(tuple(size), lambda i: tuple(i if n == cut else 0 for n in range(len(shape))))
-
-    specs = [spec(shape, cut) for (shape, _), cut in zip(arrays, blocks)]
-    n_in = len(args) - n_scalar
+def call(kernel, outs, args, n_scalar=0, scratch=(), keep=True):
+    vmem = pl.BlockSpec(memory_space=pltpu.VMEM)
+    smem = pl.BlockSpec(memory_space=pltpu.SMEM)
+    make = pltpu.VMEM if keep else jax.ShapeDtypeStruct
+    held = [pltpu.with_memory_space_constraint(a, pltpu.VMEM) for a in args[n_scalar:]]
     return pl.pallas_call(
         kernel,
-        grid=(steps,),
-        out_shape=[jax.ShapeDtypeStruct(s, d) for s, d in outs],
-        in_specs=[pl.BlockSpec(memory_space=pltpu.SMEM)] * n_scalar + specs[:n_in],
-        out_specs=specs[n_in:],
+        out_shape=[make(s, d) for s, d in outs],
+        in_specs=[smem] * n_scalar + [vmem] * len(held),
+        out_specs=[vmem] * len(outs),
         scratch_shapes=scratch,
         compiler_params=pltpu.CompilerParams(vmem_limit_bytes=VMEM_LIMIT),
-    )(*args)
+    )(*args[:n_scalar], *held)
 
 
 def take_blocks(order, source, target):
@@ -70,10 +64,7 @@
 def partial_kernel(dim, order, left, *refs):
     *weights, keep, send1, send2, send3, mine = refs
 
-    @pl.when(pl.program_id(0) == 0)
-    def _():
-        take_blocks(order, left, mine)
-
+    take_blocks(order, left, mine)
     group = keep.shape[1]
     for n, weight in enumerate(weights):
         value = contract(mine[...], weight[...], 1, dim)
@@ -126,34 +117,24 @@
 
 
 def product_kernel(dim, place, *refs):
-    pieces, weights = refs[:SIDE], refs[SIDE:-4]
-    mine, theirs, total, stack = refs[-4:]
-    tokens = stack.shape[0]
-    rows = tokens // BLOCKS
-    step = pl.program_id(0)
+    pieces, weights = refs[:SIDE], refs[SIDE:-3]
+    mine, theirs, stack = refs[-3:]
+    rows = stack.shape[0] // BLOCKS
     value = None
     for n, weight in enumerate(weights):
         stack_rows(pieces, n, stack)
         term = contract(stack[...], weight[...], 1, dim)
         value = term if value is None else value + term
-
-    @pl.when(step == 0)
-    def _():
-        total[...] = value
-
-    @pl.when(step == 1)
-    def _():
-        for s in range(BLOCKS):
-            to = place[s]
-            done = total[s * rows : (s + 1) * rows] + value[s * rows : (s + 1) * rows]
-
-            @pl.when(to < DEEP)
-            def _():
-                mine[pl.ds(pl.multiple_of(to * rows, rows), rows), :] = done
-
-            @pl.when(to >= DEEP)
-            def _():
-                theirs[pl.ds(pl.multiple_of((to - DEEP) * rows, rows), rows), :] = done
+    for s in range(BLOCKS):
+        to, block = place[s], value[s * rows : (s + 1) * rows]
+
+        @pl.when(to < DEEP)
+        def _():
+            mine[pl.ds(pl.multiple_of(to * rows, rows), rows), :] = block
+
+        @pl.when(to >= DEEP)
+        def _():
+            theirs[pl.ds(pl.multiple_of((to - DEEP) * rows, rows), rows), :] = block
 
 
 def down_grad_kernel(order, og, *refs):
@@ -210,22 +191,18 @@
         return call(
             functools.partial(partial_kernel, dim),
             [((n, group, width), F32)] + [((n, group, width), BF16)] * 3,
+            (order, left, *weights),
             1,
-            (order, left, *weights),
             [pltpu.VMEM((tokens, deep), BF16)],
-            [None] + [1 - dim] * n + [2] * 4,
-            2,
         )
 
     def product(pieces, weights, dim):
         return call(
             functools.partial(product_kernel, dim),
             [((tokens // 2, deep), F32)] * 2,
+            (place, *pieces, *weights),
             1,
-            (place, *pieces, *weights),
-            [pltpu.VMEM((tokens, deep), F32), pltpu.VMEM((tokens, width // 2), BF16)],
-            [2] * 4 + [dim] * len(weights) + [None] * 2,
-            2,
+            [pltpu.VMEM((tokens, width), BF16)],
         )
 
     keep_gu, *sends = partials(all_inputs, (gate_weight, up_weight), 0)
@@ -240,15 +217,12 @@
         return call(
             first_sum_kernel,
             [((n, rows, width), F32)] + [((n, rows, width), BF16)] * 3,
-            0,
             (keep, *got),
-            blocks=[2] * 8,
-            steps=2,
         )
 
     def join(blocks):
         n = blocks[0].shape[0]
-        (out,) = call(join_kernel, [((n, group, width), BF16)], 0, blocks, blocks=[2] * 5, steps=2)
+        (out,) = call(join_kernel, [((n, group, width), BF16)], blocks)
         return out
 
     own_gu, *sends = first_sum(keep_gu, got_gu)
@@ -258,20 +232,10 @@
     hidden, factors = call(
         hidden_kernel,
         [((1, rows, width), BF16), ((2, rows, width), F32)],
-        0,
         (own_gu, *got_gu),
-        blocks=[2] * 6,
-        steps=2,
     )
     blocks_hidden = collect(hidden, MINOR)
-    (parts,) = call(
-        parts_kernel,
-        [((2, rows, width), BF16)],
-        0,
-        (factors, own_h, *got_h),
-        blocks=[2] * 6,
-        steps=2,
-    )
+    (parts,) = call(parts_kernel, [((2, rows, width), BF16)], (factors, own_h, *got_h))
     blocks_parts = collect(parts, MINOR)
     hiddens = collect(join(blocks_hidden), MAJOR)
     grads = collect(join(blocks_parts), MAJOR)
@@ -280,14 +244,14 @@
     sums = product(hiddens, (down_weight,), 0)
     output = z_reduce(*sums, BF16, same_core)
     (down_grad,) = call(
-        down_grad_kernel, [((width, deep), BF16)], 1,
-        (order, all_grads, *hiddens), scratch,
+        down_grad_kernel, [((width, deep), BF16)], (order, all_grads, *hiddens),
+        1, scratch, keep=False,
     )
     sums = product(grads, (gate_weight, up_weight), 1)
     in_grad = z_reduce(*sums, BF16, same_core)
     gate_grad, up_grad = call(
-        weight_grads_kernel, [((deep, width), BF16)] * 2, 1,
-        (order, all_inputs, *grads), scratch,
+        weight_grads_kernel, [((deep, width), BF16)] * 2, (order, all_inputs, *grads),
+        1, scratch, keep=False,
     )
     return (output, in_grad, gate_grad, up_grad, down_grad)
 

time: 215 us -> 193 us (0.90)
  Pallas kernels: 42.7 us -> 17.8 us
  starting transfers between devices: 39.6 us -> 49 us
  waiting for transfers between devices: 79 us -> 73.5 us
  blocking collectives: 40.2 us -> 37.4 us
  other arithmetic: 3.4 us -> 6 us
    pallas_call x12, Pallas kernels: 42.7 us -> 17.8 us  [call(): pl.pallas_call(kernel, out_shape=[make(s, d) for s, d in outs], in_specs=...]
    ppermute x24, starting transfers between devices: 31.5 us -> 40.1 us  [send(): return lax.ppermute(value, ('row', 'col'), shift(k, along))]
    ppermute x24, waiting for transfers between devices: 65.3 us -> 62.4 us  [send(): return lax.ppermute(value, ('row', 'col'), shift(k, along))]
    all_to_all x2, waiting for transfers between devices: 13.6 us -> 11 us  [z_reduce(): lax.all_to_all(total, 'col', 0, 0, axis_index_groups=same_core, tiled=True)]
    unnamed x56 -> x34, local copies, waits for them, and re-layouts: 6.61 us -> 6.09 us
  transfers between devices with their start and end apart: 28 -> 28, of which waited for: 14 -> 15; matrix products, arithmetic and copies ran while one was open for 1% -> 2% of each run, Pallas kernels for 16% -> 8%
where the time goes in v3:
time: 193 us; the launch traced here: 191 us
  waiting for transfers between devices  73.5 us (38%)
  starting transfers between devices  49 us (25%)
  blocking collectives  37.4 us (19%)
  Pallas kernels  17.8 us (9%)
  local copies, waits for them, and re-layouts  6.09 us (3%)
  other arithmetic  6 us (3%)
    ppermute x24, waiting for transfers between devices, send(): return lax.ppermute(value, ('row', 'col'), shift(k, along))  62.4 us
    ppermute x24, starting transfers between devices, send(): return lax.ppermute(value, ('row', 'col'), shift(k, along))  40.1 us
    all_gather x1, blocking collectives, on_device(): all_inputs = lax.all_gather(inputs, 'col', axis=0, tiled=True)  21.7 us
    pallas_call x12, Pallas kernels, call(): pl.pallas_call(kernel, out_shape=[make(s, d) for s, d in outs], in_specs=...  17.8 us
    all_gather x1, blocking collectives, on_device(): all_grads = lax.all_gather(out_grad, 'col', axis=0, tiled=True)  15.7 us
    all_to_all x2, waiting for transfers between devices, z_reduce(): lax.all_to_all(total, 'col', 0, 0, axis_index_groups=same_core, tiled=True)  11 us
    all_to_all x2, starting transfers between devices, z_reduce(): lax.all_to_all(total, 'col', 0, 0, axis_index_groups=same_core, tiled=True)  8.7 us
    unnamed x34, local copies, waits for them, and re-layouts  6.09 us
  transfers between devices with their start and end apart: 28, of which 15 were waited for; matrix products, arithmetic and copies ran while one was open for 2% of the time, Pallas kernels for 8%

profile of v3, /device:TPU:2, one launch (start us, length us, event | category | flops | bytes accessed | tf_op | source)
XLA Modules:
  0.0 190.7 jit_solution(8233169088263369863)
XLA Ops:
  0.7 21.7 %all_gather.6.left.x = bf16[512,512]{1,0:T(8,128)(2,1)S(1)} all-gather(bf16[32,512]{1,0:T(8,128)(2,1)} %param.5), channel_id=1, replica_groups=mesh['row'=16,'col'=16] {'col'}, dimensions={0}, use_global_device_ids=true | all-gather | bytes 557056 | tf_op jit(solution)/shard_map/all_gather | solution.py:184
  22.4 1.5 copy-done.1
  23.8 1.5 copy-done.3
  25.3 2.6 %shard_map.92 = (f32[2,128,1792]{2,1,0:T(8,128)S(1)}, bf16[2,128,1792]{2,1,0:T(8,128)(2,1)S(1)}, bf16[2,128,1792]{2,1,0:T(8,128)(2,1)S(1)}, bf16[2,128,1792]{2,1,0:T(8,128)(2,1)S(1)}) custom-call(s32[16]{0:T(128)S(1)} %get-tuple-element.58.order, bf16[512,512]{1,0:T(8,128)(2,1)S(1)} %all_gather.6.left.x, bf16[512,1792]{1,0:T(8,128)(2,1)S(1)} %copy-done.1, ...), custom_call_target="tpu_custom_call" | custom-call | tf_op jit(solution)/shard_map/pallas_call | solution.py:47
  28.0 1.6 collective-permute-start
  29.5 1.1 collective-permute-start.1
  30.6 2.2 %collective-permute-start.2 = (bf16[2,128,1792]{2,1,0:T(8,128)(2,1)S(1)}, bf16[2,128,1792]{2,1,0:T(8,128)(2,1)S(1)}, u32[]{:S(2)}, u32[]{:S(2)}) collective-permute-start(bf16[2,128,1792]{2,1,0:T(8,128)(2,1)S(1)} %get-tuple-element.35), channel_id=1, source_target_pairs={{0,48},{1,193},{2,50},{3,195},{4,52},{5,197},{6,54},{7,199},{8,56}... | collective-permute-start | bytes 2752520 | tf_op jit(solution)/shard_map/ppermute | solution.py:156
  32.8 8.6 %collective-permute-done.got1 = bf16[2,128,1792]{2,1,0:T(8,128)(2,1)S(1)} collective-permute-done((bf16[2,128,1792]{2,1,0:T(8,128)(2,1)S(1)}, bf16[2,128,1792]{2,1,0:T(8,128)(2,1)S(1)}, u32[]{:S(2)}, u32[]{:S(2)}) %collective-permute-start) | collective-permute-done | bytes 917536 | tf_op jit(solution)/shard_map/ppermute | solution.py:156
  41.4 3.1 %collective-permute-done.1.got2 = bf16[2,128,1792]{2,1,0:T(8,128)(2,1)S(1)} collective-permute-done((bf16[2,128,1792]{2,1,0:T(8,128)(2,1)S(1)}, bf16[2,128,1792]{2,1,0:T(8,128)(2,1)S(1)}, u32[]{:S(2)}, u32[]{:S(2)}) %collective-permute-start.1) | collective-permute-done | bytes 917536 | tf_op jit(solution)/shard_map/ppermute | solution.py:156
  44.5 9.3 %collective-permute-done.2.got3 = bf16[2,128,1792]{2,1,0:T(8,128)(2,1)S(1)} collective-permute-done((bf16[2,128,1792]{2,1,0:T(8,128)(2,1)S(1)}, bf16[2,128,1792]{2,1,0:T(8,128)(2,1)S(1)}, u32[]{:S(2)}, u32[]{:S(2)}) %collective-permute-start.2) | collective-permute-done | bytes 917536 | tf_op jit(solution)/shard_map/ppermute | solution.py:156
  54.3 1.7 collective-permute-start.3
  55.9 2.9 %collective-permute-start.4 = (bf16[2,32,1792]{2,1,0:T(8,128)(2,1)S(1)}, bf16[2,32,1792]{2,1,0:T(8,128)(2,1)S(1)}, u32[]{:S(2)}, u32[]{:S(2)}) collective-permute-start(bf16[2,32,1792]{2,1,0:T(8,128)(2,1)S(1)} %get-tuple-element.38), channel_id=1, source_target_pairs={{0,128},{1,33},{2,130},{3,35},{4,132},{5,37},{6,134},{7,39},{8,136... | collective-permute-start | bytes 688136 | tf_op jit(solution)/shard_map/ppermute | solution.py:156
  58.8 1.3 collective-permute-start.5
  60.2 15.7 %all_gather.7.left.og = bf16[512,512]{1,0:T(8,128)(2,1)S(1)} all-gather(bf16[32,512]{1,0:T(8,128)(2,1)S(1)} %copy-done.16), channel_id=1, replica_groups=mesh['row'=16,'col'=16] {'col'}, dimensions={0}, use_global_device_ids=true | all-gather | bytes 557056 | tf_op jit(solution)/shard_map/all_gather | solution.py:211
  75.9 1.7 shard_map.97
  77.6 1.1 collective-permute-start.13
  78.6 1.2 collective-permute-start.14
  79.8 1.9 %collective-permute-start.15 = (bf16[1,128,1792]{2,1,0:T(8,128)(2,1)S(1)}, bf16[1,128,1792]{2,1,0:T(8,128)(2,1)S(1)}, u32[]{:S(2)}, u32[]{:S(2)}) collective-permute-start(bf16[1,128,1792]{2,1,0:T(8,128)(2,1)S(1)} %get-tuple-element.48), channel_id=1, source_target_pairs={{0,48},{1,193},{2,50},{3,195},{4,52},{5,197},{6,54},{7,199},{8,56}... | collective-permute-start | bytes 1376264 | tf_op jit(solution)/shard_map/ppermute | solution.py:156
  82.1 2.7 %collective-permute-start.7 = (bf16[1,32,1792]{2,1,0:T(8,128)(2,1)S(1)}, bf16[1,32,1792]{2,1,0:T(8,128)(2,1)S(1)}, u32[]{:S(2)}, u32[]{:S(2)}) collective-permute-start(bf16[1,32,1792]{2,1,0:T(8,128)(2,1)S(1)} %get-tuple-element.40.refs_0_), channel_id=1, source_target_pairs={{0,128},{1,33},{2,130},{3,35},{4,132},{5,37},{6,134},{7,39},{8,136... | collective-permute-start | bytes 344072 | tf_op jit(solution)/shard_map/ppermute | solution.py:156
  84.8 5.1 %collective-permute-done.6.refs_1_ = bf16[1,32,1792]{2,1,0:T(8,128)(2,1)S(1)} collective-permute-done((bf16[1,32,1792]{2,1,0:T(8,128)(2,1)S(1)}, bf16[1,32,1792]{2,1,0:T(8,128)(2,1)S(1)}, u32[]{:S(2)}, u32[]{:S(2)}) %collective-permute-start.6) | collective-permute-done | bytes 114720 | tf_op jit(solution)/shard_map/ppermute | solution.py:156
  89.9 2.0 %collective-permute-start.8 = (bf16[1,32,1792]{2,1,0:T(8,128)(2,1)S(1)}, bf16[1,32,1792]{2,1,0:T(8,128)(2,1)S(1)}, u32[]{:S(2)}, u32[]{:S(2)}) collective-permute-start(bf16[1,32,1792]{2,1,0:T(8,128)(2,1)S(1)} %get-tuple-element.40.refs_0_), channel_id=1, source_target_pairs={{0,64},{1,17},{2,66},{3,19},{4,68},{5,21},{6,70},{7,23},{8,72},{9,... | collective-permute-start | bytes 344072 | tf_op jit(solution)/shard_map/ppermute | solution.py:156
  91.9 4.6 %collective-permute-done.8.refs_3_ = bf16[1,32,1792]{2,1,0:T(8,128)(2,1)S(1)} collective-permute-done((bf16[1,32,1792]{2,1,0:T(8,128)(2,1)S(1)}, bf16[1,32,1792]{2,1,0:T(8,128)(2,1)S(1)}, u32[]{:S(2)}, u32[]{:S(2)}) %collective-permute-start.8) | collective-permute-done | bytes 114720 | tf_op jit(solution)/shard_map/ppermute | solution.py:156
  97.3 3.3 %collective-permute-start.17 = (bf16[1,32,1792]{2,1,0:T(8,128)(2,1)S(1)}, bf16[1,32,1792]{2,1,0:T(8,128)(2,1)S(1)}, u32[]{:S(2)}, u32[]{:S(2)}) collective-permute-start(bf16[1,32,1792]{2,1,0:T(8,128)(2,1)S(1)} %get-tuple-element.51), channel_id=1, source_target_pairs={{0,128},{1,33},{2,130},{3,35},{4,132},{5,37},{6,134},{7,39},{8,136... | collective-permute-start | bytes 344072 | tf_op jit(solution)/shard_map/ppermute | solution.py:156
  100.8 2.3 %collective-permute-done.16.refs_1_ = bf16[1,32,1792]{2,1,0:T(8,128)(2,1)S(1)} collective-permute-done((bf16[1,32,1792]{2,1,0:T(8,128)(2,1)S(1)}, bf16[1,32,1792]{2,1,0:T(8,128)(2,1)S(1)}, u32[]{:S(2)}, u32[]{:S(2)}) %collective-permute-start.16) | collective-permute-done | bytes 114720 | tf_op jit(solution)/shard_map/ppermute | solution.py:156
  103.1 1.5 collective-permute-done.17.refs_2_
  104.6 2.0 %collective-permute-done.18.refs_3_ = bf16[1,32,1792]{2,1,0:T(8,128)(2,1)S(1)} collective-permute-done((bf16[1,32,1792]{2,1,0:T(8,128)(2,1)S(1)}, bf16[1,32,1792]{2,1,0:T(8,128)(2,1)S(1)}, u32[]{:S(2)}, u32[]{:S(2)}) %collective-permute-start.18) | collective-permute-done | bytes 114720 | tf_op jit(solution)/shard_map/ppermute | solution.py:156
  106.7 1.6 collective-permute-start.19
  108.3 1.0 collective-permute-start.20
  109.3 2.2 %collective-permute-start.10 = (bf16[1,128,1792]{2,1,0:T(8,128)(2,1)S(1)}, bf16[1,128,1792]{2,1,0:T(8,128)(2,1)S(1)}, u32[]{:S(2)}, u32[]{:S(2)}) collective-permute-start(bf16[1,128,1792]{2,1,0:T(8,128)(2,1)S(1)} %shard_map.95.refs_0_), channel_id=1, source_target_pairs={{0,32},{1,129},{2,34},{3,131},{4,36},{5,133},{6,38},{7,135},{8,40}... | collective-permute-start | bytes 1376264 | tf_op jit(solution)/shard_map/ppermute | solution.py:156
  111.5 1.9 collective-permute-done.19.refs_1_
  113.4 8.5 %collective-permute-start.11 = (bf16[1,128,1792]{2,1,0:T(8,128)(2,1)S(1)}, bf16[1,128,1792]{2,1,0:T(8,128)(2,1)S(1)}, u32[]{:S(2)}, u32[]{:S(2)}) collective-permute-start(bf16[1,128,1792]{2,1,0:T(8,128)(2,1)S(1)} %shard_map.95.refs_0_), channel_id=1, source_target_pairs={{0,16},{1,65},{2,18},{3,67},{4,20},{5,69},{6,22},{7,71},{8,24},{9,... | collective-permute-start | bytes 1376264 | tf_op jit(solution)/shard_map/ppermute | solution.py:156
  121.9 3.7 %collective-permute-done.21.refs_3_ = bf16[2,32,1792]{2,1,0:T(8,128)(2,1)S(1)} collective-permute-done((bf16[2,32,1792]{2,1,0:T(8,128)(2,1)S(1)}, bf16[2,32,1792]{2,1,0:T(8,128)(2,1)S(1)}, u32[]{:S(2)}, u32[]{:S(2)}) %collective-permute-start.21) | collective-permute-done | bytes 229408 | tf_op jit(solution)/shard_map/ppermute | solution.py:156
  126.0 2.6 %collective-permute-start.23 = (bf16[2,128,1792]{2,1,0:T(8,128)(2,1)S(1)}, bf16[2,128,1792]{2,1,0:T(8,128)(2,1)S(1)}, u32[]{:S(2)}, u32[]{:S(2)}) collective-permute-start(bf16[2,128,1792]{2,1,0:T(8,128)(2,1)S(1)} %shard_map.100.refs_0_), channel_id=1, source_target_pairs={{0,32},{1,129},{2,34},{3,131},{4,36},{5,133},{6,38},{7,135},{8,40}... | collective-permute-start | bytes 2752520 | tf_op jit(solution)/shard_map/ppermute | solution.py:156
  128.7 1.9 shard_map.96
  130.7 8.3 %collective-permute-done.22.refs_1_ = bf16[2,128,1792]{2,1,0:T(8,128)(2,1)S(1)} collective-permute-done((bf16[2,128,1792]{2,1,0:T(8,128)(2,1)S(1)}, bf16[2,128,1792]{2,1,0:T(8,128)(2,1)S(1)}, u32[]{:S(2)}, u32[]{:S(2)}) %collective-permute-start.22) | collective-permute-done | bytes 917536 | tf_op jit(solution)/shard_map/ppermute | solution.py:156
  139.1 10.7 %collective-permute-done.23.refs_2_ = bf16[2,128,1792]{2,1,0:T(8,128)(2,1)S(1)} collective-permute-done((bf16[2,128,1792]{2,1,0:T(8,128)(2,1)S(1)}, bf16[2,128,1792]{2,1,0:T(8,128)(2,1)S(1)}, u32[]{:S(2)}, u32[]{:S(2)}) %collective-permute-start.23) | collective-permute-done | bytes 917536 | tf_op jit(solution)/shard_map/ppermute | solution.py:156
  149.8 1.2 collective-permute-done.24.refs_3_
  151.0 3.7 %shard_map.101 = (f32[256,512]{1,0:T(8,128)S(1)}, f32[256,512]{1,0:T(8,128)}) custom-call(s32[16]{0:T(128)S(1)} %get-tuple-element.57.place, bf16[2,128,1792]{2,1,0:T(8,128)(2,1)S(1)} %shard_map.100.refs_0_, bf16[2,128,1792]{2,1,0:T(8,128)(2,1)S(1)} %collective-permute-done.22.refs_1_, bf16[2,128,1792]{2,1,0:T(8,128)(2,1)S(1)} %collective-permute-done.23.refs_2_, ...), custom_call_target="tpu_custom_call" | custom-call | tf_op jit(solution)/shard_map/pallas_call | solution.py:47
  155.6 4.4 %all-to-all-start = ((bf16[8,32,512]{2,1,0:T(8,128)(2,1)}), bf16[8,32,512]{2,1,0:T(8,128)(2,1)}, u32[]{:S(2)}, u32[]{:S(2)}) async-start(bf16[8,32,512]{2,1,0:T(8,128)(2,1)} %bitcast.3), calls=%async_computation | async-start | bytes 524288 | tf_op jit(solution)/shard_map/all_to_all | solution.py:169
  160.0 2.0 %add_convert_fusion = bf16[256,512]{1,0:T(8,128)(2,1)} fusion(f32[256,512]{1,0:T(8,128)} %copy-done.15, f32[256,512]{1,0:T(8,128)} %collective-permute-done.25), kind=kLoop, calls=%fused_computation | loop fusion | flops 262144 | bytes 1310720 | tf_op jit(solution)/shard_map/convert_element_type | solution.py:168
  162.0 10.6 %all-to-all-done = bf16[8,32,512]{2,1,0:T(8,128)(2,1)} async-done(((bf16[8,32,512]{2,1,0:T(8,128)(2,1)}), bf16[8,32,512]{2,1,0:T(8,128)(2,1)}, u32[]{:S(2)}, u32[]{:S(2)}) %all-to-all-start) | async-done | bytes 262176 | tf_op jit(solution)/shard_map/all_to_all | solution.py:169
  172.7 4.3 %all-to-all-start.1 = ((bf16[8,32,512]{2,1,0:T(8,128)(2,1)}), bf16[8,32,512]{2,1,0:T(8,128)(2,1)}, u32[]{:S(2)}, u32[]{:S(2)}) async-start(bf16[8,32,512]{2,1,0:T(8,128)(2,1)} %bitcast.2), calls=%async_computation.1 | async-start | bytes 524288 | tf_op jit(solution)/shard_map/all_to_all | solution.py:169
  178.0 1.0 copy-done.12
  179.0 1.0 copy-done.14
  180.0 2.9 %shard_map.103 = bf16[1792,512]{1,0:T(8,128)(2,1)} custom-call(s32[16]{0:T(128)S(1)} %get-tuple-element.58.order, bf16[512,512]{1,0:T(8,128)(2,1)S(1)} %all_gather.7.left.og, bf16[1,128,1792]{2,1,0:T(8,128)(2,1)S(1)} %shard_map.95.refs_0_, bf16[1,128,1792]{2,1,0:T(8,128)(2,1)S(1)} %copy-done.10, bf16[1,128,1792]{2,1,0:T(8,128)(2,1)S(1)} %copy-done.12, ...), custom_call_target="tpu_custom_call" | custom-call | tf_op jit(solution)/shard_map/pallas_call | solution.py:47
  182.9 4.2 %shard_map.102 = (bf16[512,1792]{1,0:T(8,128)(2,1)}, bf16[512,1792]{1,0:T(8,128)(2,1)}) custom-call(s32[16]{0:T(128)S(1)} %get-tuple-element.58.order, bf16[512,512]{1,0:T(8,128)(2,1)S(1)} %all_gather.6.left.x, bf16[2,128,1792]{2,1,0:T(8,128)(2,1)S(1)} %shard_map.100.refs_0_, bf16[2,128,1792]{2,1,0:T(8,128)(2,1)S(1)} %collective-permute-done.22.refs_1_, ...), custom_call_target="tpu_custom_call" | custom-call | tf_op jit(solution)/shard_map/pallas_call | solution.py:47
  187.1 1.6 reduce_sum.24
  189.1 1.6 reduce_sum.25
  (61 shorter events, 4.7 us)
Async XLA Ops:
  22.3 1.5 copy-start.1
  23.8 1.5 copy-start.3
  28.0 13.5 %collective-permute-start = (bf16[2,128,1792]{2,1,0:T(8,128)(2,1)S(1)}, bf16[2,128,1792]{2,1,0:T(8,128)(2,1)S(1)}, u32[]{:S(2)}, u32[]{:S(2)}) collective-permute-start(bf16[2,128,1792]{2,1,0:T(8,128)(2,1)S(1)} %get-tuple-element.33), channel_id=1, source_target_pairs={{0,16},{1,65},{2,18},{3,67},{4,20},{5,69},{6,22},{7,71},{8,24},{9,... | collective-permute-start | bytes 2752520 | tf_op jit(solution)/shard_map/ppermute | solution.py:156
  29.5 15.0 %collective-permute-start.1 = (bf16[2,128,1792]{2,1,0:T(8,128)(2,1)S(1)}, bf16[2,128,1792]{2,1,0:T(8,128)(2,1)S(1)}, u32[]{:S(2)}, u32[]{:S(2)}) collective-permute-start(bf16[2,128,1792]{2,1,0:T(8,128)(2,1)S(1)} %get-tuple-element.34), channel_id=1, source_target_pairs={{0,32},{1,129},{2,34},{3,131},{4,36},{5,133},{6,38},{7,135},{8,40}... | collective-permute-start | bytes 2752520 | tf_op jit(solution)/shard_map/ppermute | solution.py:156
  30.6 23.2 %collective-permute-start.2 = (bf16[2,128,1792]{2,1,0:T(8,128)(2,1)S(1)}, bf16[2,128,1792]{2,1,0:T(8,128)(2,1)S(1)}, u32[]{:S(2)}, u32[]{:S(2)}) collective-permute-start(bf16[2,128,1792]{2,1,0:T(8,128)(2,1)S(1)} %get-tuple-element.35), channel_id=1, source_target_pairs={{0,48},{1,193},{2,50},{3,195},{4,52},{5,197},{6,54},{7,199},{8,56}... | collective-permute-start | bytes 2752520 | tf_op jit(solution)/shard_map/ppermute | solution.py:156
  32.8 27.4 %copy-start.16 = (bf16[32,512]{1,0:T(8,128)(2,1)S(1)}, bf16[32,512]{1,0:T(8,128)(2,1)}, u32[]{:S(2)}) copy-start(bf16[32,512]{1,0:T(8,128)(2,1)} %param.9) | copy-start | bytes 98308
  32.8 43.1 %copy-start = (bf16[1792,512]{1,0:T(8,128)(2,1)S(1)}, bf16[1792,512]{1,0:T(8,128)(2,1)}, u32[]{:S(2)}) copy-start(bf16[1792,512]{1,0:T(8,128)(2,1)} %refs_0_.3) | copy-start | bytes 5505028
  54.3 25.6 %collective-permute-start.3 = (bf16[2,32,1792]{2,1,0:T(8,128)(2,1)S(1)}, bf16[2,32,1792]{2,1,0:T(8,128)(2,1)S(1)}, u32[]{:S(2)}, u32[]{:S(2)}) collective-permute-start(bf16[2,32,1792]{2,1,0:T(8,128)(2,1)S(1)} %get-tuple-element.37), channel_id=1, source_target_pairs={{0,64},{1,17},{2,66},{3,19},{4,68},{5,21},{6,70},{7,23},{8,72},{9,... | collective-permute-start | bytes 688136 | tf_op jit(solution)/shard_map/ppermute | solution.py:156
  55.9 25.9 %collective-permute-start.4 = (bf16[2,32,1792]{2,1,0:T(8,128)(2,1)S(1)}, bf16[2,32,1792]{2,1,0:T(8,128)(2,1)S(1)}, u32[]{:S(2)}, u32[]{:S(2)}) collective-permute-start(bf16[2,32,1792]{2,1,0:T(8,128)(2,1)S(1)} %get-tuple-element.38), channel_id=1, source_target_pairs={{0,128},{1,33},{2,130},{3,35},{4,132},{5,37},{6,134},{7,39},{8,136... | collective-permute-start | bytes 688136 | tf_op jit(solution)/shard_map/ppermute | solution.py:156
  58.8 23.0 %collective-permute-start.5 = (bf16[2,32,1792]{2,1,0:T(8,128)(2,1)S(1)}, bf16[2,32,1792]{2,1,0:T(8,128)(2,1)S(1)}, u32[]{:S(2)}, u32[]{:S(2)}) collective-permute-start(bf16[2,32,1792]{2,1,0:T(8,128)(2,1)S(1)} %get-tuple-element.39), channel_id=1, source_target_pairs={{0,192},{1,49},{2,194},{3,51},{4,196},{5,53},{6,198},{7,55},{8,200... | collective-permute-start | bytes 688136 | tf_op jit(solution)/shard_map/ppermute | solution.py:156
  77.6 19.3 %collective-permute-start.13 = (bf16[1,128,1792]{2,1,0:T(8,128)(2,1)S(1)}, bf16[1,128,1792]{2,1,0:T(8,128)(2,1)S(1)}, u32[]{:S(2)}, u32[]{:S(2)}) collective-permute-start(bf16[1,128,1792]{2,1,0:T(8,128)(2,1)S(1)} %get-tuple-element.46), channel_id=1, source_target_pairs={{0,16},{1,65},{2,18},{3,67},{4,20},{5,69},{6,22},{7,71},{8,24},{9,... | collective-permute-start | bytes 1376264 | tf_op jit(solution)/shard_map/ppermute | solution.py:156
  78.6 18.2 %collective-permute-start.14 = (bf16[1,128,1792]{2,1,0:T(8,128)(2,1)S(1)}, bf16[1,128,1792]{2,1,0:T(8,128)(2,1)S(1)}, u32[]{:S(2)}, u32[]{:S(2)}) collective-permute-start(bf16[1,128,1792]{2,1,0:T(8,128)(2,1)S(1)} %get-tuple-element.47), channel_id=1, source_target_pairs={{0,32},{1,129},{2,34},{3,131},{4,36},{5,133},{6,38},{7,135},{8,40}... | collective-permute-start | bytes 1376264 | tf_op jit(solution)/shard_map/ppermute | solution.py:156
  79.8 17.0 %collective-permute-start.15 = (bf16[1,128,1792]{2,1,0:T(8,128)(2,1)S(1)}, bf16[1,128,1792]{2,1,0:T(8,128)(2,1)S(1)}, u32[]{:S(2)}, u32[]{:S(2)}) collective-permute-start(bf16[1,128,1792]{2,1,0:T(8,128)(2,1)S(1)} %get-tuple-element.48), channel_id=1, source_target_pairs={{0,48},{1,193},{2,50},{3,195},{4,52},{5,197},{6,54},{7,199},{8,56}... | collective-permute-start | bytes 1376264 | tf_op jit(solution)/shard_map/ppermute | solution.py:156
  82.0 7.9 %collective-permute-start.6 = (bf16[1,32,1792]{2,1,0:T(8,128)(2,1)S(1)}, bf16[1,32,1792]{2,1,0:T(8,128)(2,1)S(1)}, u32[]{:S(2)}, u32[]{:S(2)}) collective-permute-start(bf16[1,32,1792]{2,1,0:T(8,128)(2,1)S(1)} %get-tuple-element.40.refs_0_), channel_id=1, source_target_pairs={{0,192},{1,49},{2,194},{3,51},{4,196},{5,53},{6,198},{7,55},{8,200... | collective-permute-start | bytes 344072 | tf_op jit(solution)/shard_map/ppermute | solution.py:156
  82.1 9.9 %collective-permute-start.7 = (bf16[1,32,1792]{2,1,0:T(8,128)(2,1)S(1)}, bf16[1,32,1792]{2,1,0:T(8,128)(2,1)S(1)}, u32[]{:S(2)}, u32[]{:S(2)}) collective-permute-start(bf16[1,32,1792]{2,1,0:T(8,128)(2,1)S(1)} %get-tuple-element.40.refs_0_), channel_id=1, source_target_pairs={{0,128},{1,33},{2,130},{3,35},{4,132},{5,37},{6,134},{7,39},{8,136... | collective-permute-start | bytes 344072 | tf_op jit(solution)/shard_map/ppermute | solution.py:156
  89.9 6.6 %collective-permute-start.8 = (bf16[1,32,1792]{2,1,0:T(8,128)(2,1)S(1)}, bf16[1,32,1792]{2,1,0:T(8,128)(2,1)S(1)}, u32[]{:S(2)}, u32[]{:S(2)}) collective-permute-start(bf16[1,32,1792]{2,1,0:T(8,128)(2,1)S(1)} %get-tuple-element.40.refs_0_), channel_id=1, source_target_pairs={{0,64},{1,17},{2,66},{3,19},{4,68},{5,21},{6,70},{7,23},{8,72},{9,... | collective-permute-start | bytes 344072 | tf_op jit(solution)/shard_map/ppermute | solution.py:156
  96.5 32.1 %collective-permute-start.9 = (bf16[1,128,1792]{2,1,0:T(8,128)(2,1)S(1)}, bf16[1,128,1792]{2,1,0:T(8,128)(2,1)S(1)}, u32[]{:S(2)}, u32[]{:S(2)}) collective-permute-start(bf16[1,128,1792]{2,1,0:T(8,128)(2,1)S(1)} %shard_map.95.refs_0_), channel_id=1, source_target_pairs={{0,48},{1,193},{2,50},{3,195},{4,52},{5,197},{6,54},{7,199},{8,56}... | collective-permute-start | bytes 1376264 | tf_op jit(solution)/shard_map/ppermute | solution.py:156
  97.0 6.1 %collective-permute-start.16 = (bf16[1,32,1792]{2,1,0:T(8,128)(2,1)S(1)}, bf16[1,32,1792]{2,1,0:T(8,128)(2,1)S(1)}, u32[]{:S(2)}, u32[]{:S(2)}) collective-permute-start(bf16[1,32,1792]{2,1,0:T(8,128)(2,1)S(1)} %get-tuple-element.50), channel_id=1, source_target_pairs={{0,64},{1,17},{2,66},{3,19},{4,68},{5,21},{6,70},{7,23},{8,72},{9,... | collective-permute-start | bytes 344072 | tf_op jit(solution)/shard_map/ppermute | solution.py:156
  97.3 7.3 %collective-permute-start.17 = (bf16[1,32,1792]{2,1,0:T(8,128)(2,1)S(1)}, bf16[1,32,1792]{2,1,0:T(8,128)(2,1)S(1)}, u32[]{:S(2)}, u32[]{:S(2)}) collective-permute-start(bf16[1,32,1792]{2,1,0:T(8,128)(2,1)S(1)} %get-tuple-element.51), channel_id=1, source_target_pairs={{0,128},{1,33},{2,130},{3,35},{4,132},{5,37},{6,134},{7,39},{8,136... | collective-permute-start | bytes 344072 | tf_op jit(solution)/shard_map/ppermute | solution.py:156
  100.6 6.0 %collective-permute-start.18 = (bf16[1,32,1792]{2,1,0:T(8,128)(2,1)S(1)}, bf16[1,32,1792]{2,1,0:T(8,128)(2,1)S(1)}, u32[]{:S(2)}, u32[]{:S(2)}) collective-permute-start(bf16[1,32,1792]{2,1,0:T(8,128)(2,1)S(1)} %get-tuple-element.52), channel_id=1, source_target_pairs={{0,192},{1,49},{2,194},{3,51},{4,196},{5,53},{6,198},{7,55},{8,200... | collective-permute-start | bytes 344072 | tf_op jit(solution)/shard_map/ppermute | solution.py:156
  106.7 6.7 %collective-permute-start.19 = (bf16[2,32,1792]{2,1,0:T(8,128)(2,1)S(1)}, bf16[2,32,1792]{2,1,0:T(8,128)(2,1)S(1)}, u32[]{:S(2)}, u32[]{:S(2)}) collective-permute-start(bf16[2,32,1792]{2,1,0:T(8,128)(2,1)S(1)} %shard_map.99.refs_0_), channel_id=1, source_target_pairs={{0,192},{1,49},{2,194},{3,51},{4,196},{5,53},{6,198},{7,55},{8,200... | collective-permute-start | bytes 688136 | tf_op jit(solution)/shard_map/ppermute | solution.py:156
  108.3 13.6 %collective-permute-start.20 = (bf16[2,32,1792]{2,1,0:T(8,128)(2,1)S(1)}, bf16[2,32,1792]{2,1,0:T(8,128)(2,1)S(1)}, u32[]{:S(2)}, u32[]{:S(2)}) collective-permute-start(bf16[2,32,1792]{2,1,0:T(8,128)(2,1)S(1)} %shard_map.99.refs_0_), channel_id=1, source_target_pairs={{0,128},{1,33},{2,130},{3,35},{4,132},{5,37},{6,134},{7,39},{8,136... | collective-permute-start | bytes 688136 | tf_op jit(solution)/shard_map/ppermute | solution.py:156
  109.3 16.2 %collective-permute-start.21 = (bf16[2,32,1792]{2,1,0:T(8,128)(2,1)S(1)}, bf16[2,32,1792]{2,1,0:T(8,128)(2,1)S(1)}, u32[]{:S(2)}, u32[]{:S(2)}) collective-permute-start(bf16[2,32,1792]{2,1,0:T(8,128)(2,1)S(1)} %shard_map.99.refs_0_), channel_id=1, source_target_pairs={{0,64},{1,17},{2,66},{3,19},{4,68},{5,21},{6,70},{7,23},{8,72},{9,... | collective-permute-start | bytes 688136 | tf_op jit(solution)/shard_map/ppermute | solution.py:156
  109.3 19.3 %collective-permute-start.10 = (bf16[1,128,1792]{2,1,0:T(8,128)(2,1)S(1)}, bf16[1,128,1792]{2,1,0:T(8,128)(2,1)S(1)}, u32[]{:S(2)}, u32[]{:S(2)}) collective-permute-start(bf16[1,128,1792]{2,1,0:T(8,128)(2,1)S(1)} %shard_map.95.refs_0_), channel_id=1, source_target_pairs={{0,32},{1,129},{2,34},{3,131},{4,36},{5,133},{6,38},{7,135},{8,40}... | collective-permute-start | bytes 1376264 | tf_op jit(solution)/shard_map/ppermute | solution.py:156
  113.4 15.3 %collective-permute-start.11 = (bf16[1,128,1792]{2,1,0:T(8,128)(2,1)S(1)}, bf16[1,128,1792]{2,1,0:T(8,128)(2,1)S(1)}, u32[]{:S(2)}, u32[]{:S(2)}) collective-permute-start(bf16[1,128,1792]{2,1,0:T(8,128)(2,1)S(1)} %shard_map.95.refs_0_), channel_id=1, source_target_pairs={{0,16},{1,65},{2,18},{3,67},{4,20},{5,69},{6,22},{7,71},{8,24},{9,... | collective-permute-start | bytes 1376264 | tf_op jit(solution)/shard_map/ppermute | solution.py:156
  125.6 13.5 %collective-permute-start.22 = (bf16[2,128,1792]{2,1,0:T(8,128)(2,1)S(1)}, bf16[2,128,1792]{2,1,0:T(8,128)(2,1)S(1)}, u32[]{:S(2)}, u32[]{:S(2)}) collective-permute-start(bf16[2,128,1792]{2,1,0:T(8,128)(2,1)S(1)} %shard_map.100.refs_0_), channel_id=1, source_target_pairs={{0,48},{1,193},{2,50},{3,195},{4,52},{5,197},{6,54},{7,199},{8,56}... | collective-permute-start | bytes 2752520 | tf_op jit(solution)/shard_map/ppermute | solution.py:156
  126.0 23.8 %collective-permute-start.23 = (bf16[2,128,1792]{2,1,0:T(8,128)(2,1)S(1)}, bf16[2,128,1792]{2,1,0:T(8,128)(2,1)S(1)}, u32[]{:S(2)}, u32[]{:S(2)}) collective-permute-start(bf16[2,128,1792]{2,1,0:T(8,128)(2,1)S(1)} %shard_map.100.refs_0_), channel_id=1, source_target_pairs={{0,32},{1,129},{2,34},{3,131},{4,36},{5,133},{6,38},{7,135},{8,40}... | collective-permute-start | bytes 2752520 | tf_op jit(solution)/shard_map/ppermute | solution.py:156
  128.6 2.0 %copy-start.9 = (bf16[1,128,1792]{2,1,0:T(8,128)(2,1)}, bf16[1,128,1792]{2,1,0:T(8,128)(2,1)S(1)}, u32[]{:S(2)}) copy-start(bf16[1,128,1792]{2,1,0:T(8,128)(2,1)S(1)} %collective-permute-done.9.refs_1_) | copy-start | bytes 1376260
  128.6 22.4 %collective-permute-start.24 = (bf16[2,128,1792]{2,1,0:T(8,128)(2,1)S(1)}, bf16[2,128,1792]{2,1,0:T(8,128)(2,1)S(1)}, u32[]{:S(2)}, u32[]{:S(2)}) collective-permute-start(bf16[2,128,1792]{2,1,0:T(8,128)(2,1)S(1)} %shard_map.100.refs_0_), channel_id=1, source_target_pairs={{0,16},{1,65},{2,18},{3,67},{4,20},{5,69},{6,22},{7,71},{8,24},{9,... | collective-permute-start | bytes 2752520 | tf_op jit(solution)/shard_map/ppermute | solution.py:156
  128.6 2.0 %copy-start.11 = (bf16[1,128,1792]{2,1,0:T(8,128)(2,1)}, bf16[1,128,1792]{2,1,0:T(8,128)(2,1)S(1)}, u32[]{:S(2)}) copy-start(bf16[1,128,1792]{2,1,0:T(8,128)(2,1)S(1)} %collective-permute-done.10.refs_2_) | copy-start | bytes 1376260
  128.7 2.0 %copy-start.13 = (bf16[1,128,1792]{2,1,0:T(8,128)(2,1)}, bf16[1,128,1792]{2,1,0:T(8,128)(2,1)S(1)}, u32[]{:S(2)}) copy-start(bf16[1,128,1792]{2,1,0:T(8,128)(2,1)S(1)} %collective-permute-done.11.refs_3_) | copy-start | bytes 1376260
  128.7 22.4 %copy-start.2 = (bf16[512,1792]{1,0:T(8,128)(2,1)S(1)}, bf16[512,1792]{1,0:T(8,128)(2,1)}, u32[]{:S(2)}) copy-start(bf16[512,1792]{1,0:T(8,128)(2,1)} %refs_4_.3) | copy-start | bytes 5505028
  128.7 22.3 %copy-start.4 = (bf16[512,1792]{1,0:T(8,128)(2,1)S(1)}, bf16[512,1792]{1,0:T(8,128)(2,1)}, u32[]{:S(2)}) copy-start(bf16[512,1792]{1,0:T(8,128)(2,1)} %refs_5_.1) | copy-start | bytes 5505028
  130.6 24.2 %collective-permute-start.12 = (f32[256,512]{1,0:T(8,128)S(1)}, f32[256,512]{1,0:T(8,128)S(1)}, u32[]{:S(2)}, u32[]{:S(2)}) collective-permute-start(f32[256,512]{1,0:T(8,128)S(1)} %get-tuple-element.42), channel_id=1, source_target_pairs={{0,1},{1,0},{2,3},{3,2},{4,5},{5,4},{6,7},{7,6},{8,9},{9,8},{10,11... | collective-permute-start | bytes 1572872 | tf_op jit(solution)/shard_map/ppermute | solution.py:168
  149.8 4.9 %copy-start.5 = (bf16[2,128,1792]{2,1,0:T(8,128)(2,1)}, bf16[2,128,1792]{2,1,0:T(8,128)(2,1)S(1)}, u32[]{:S(2)}) copy-start(bf16[2,128,1792]{2,1,0:T(8,128)(2,1)S(1)} %collective-permute-done.23.refs_2_) | copy-start | bytes 2752516
  151.0 3.7 %copy-start.7 = (bf16[2,128,1792]{2,1,0:T(8,128)(2,1)}, bf16[2,128,1792]{2,1,0:T(8,128)(2,1)S(1)}, u32[]{:S(2)}) copy-start(bf16[2,128,1792]{2,1,0:T(8,128)(2,1)S(1)} %collective-permute-done.24.refs_3_) | copy-start | bytes 2752516
  154.7 0.9 copy-start.15
  154.7 5.3 %collective-permute-start.25 = (f32[256,512]{1,0:T(8,128)}, f32[256,512]{1,0:T(8,128)}, u32[]{:S(2)}, u32[]{:S(2)}) collective-permute-start(f32[256,512]{1,0:T(8,128)} %get-tuple-element.54), channel_id=1, source_target_pairs={{0,1},{1,0},{2,3},{3,2},{4,5},{5,4},{6,7},{7,6},{8,9},{9,8},{10,11... | collective-permute-start | bytes 1572872 | tf_op jit(solution)/shard_map/ppermute | solution.py:168
  155.6 17.0 %all-to-all-start = ((bf16[8,32,512]{2,1,0:T(8,128)(2,1)}), bf16[8,32,512]{2,1,0:T(8,128)(2,1)}, u32[]{:S(2)}, u32[]{:S(2)}) async-start(bf16[8,32,512]{2,1,0:T(8,128)(2,1)} %bitcast.3), calls=%async_computation | async-start | bytes 524288 | tf_op jit(solution)/shard_map/all_to_all | solution.py:169
  172.7 16.4 %all-to-all-start.1 = ((bf16[8,32,512]{2,1,0:T(8,128)(2,1)}), bf16[8,32,512]{2,1,0:T(8,128)(2,1)}, u32[]{:S(2)}, u32[]{:S(2)}) async-start(bf16[8,32,512]{2,1,0:T(8,128)(2,1)} %bitcast.2), calls=%async_computation.1 | async-start | bytes 524288 | tf_op jit(solution)/shard_map/all_to_all | solution.py:169
  176.9 1.0 copy-start.10
  178.0 1.0 copy-start.12
  179.0 1.0 copy-start.14
  180.0 2.9 %copy-start.6 = (bf16[2,128,1792]{2,1,0:T(8,128)(2,1)S(1)}, bf16[2,128,1792]{2,1,0:T(8,128)(2,1)}, u32[]{:S(2)}) copy-start(bf16[2,128,1792]{2,1,0:T(8,128)(2,1)} %copy-done.5) | copy-start | bytes 2752516
  180.0 2.9 %copy-start.8 = (bf16[2,128,1792]{2,1,0:T(8,128)(2,1)S(1)}, bf16[2,128,1792]{2,1,0:T(8,128)(2,1)}, u32[]{:S(2)}) copy-start(bf16[2,128,1792]{2,1,0:T(8,128)(2,1)} %copy-done.7) | copy-start | bytes 2752516
